TPU v7x, 512 devices: a whole 4x4x16 slice. The times are simulated.
512 devices in a mesh: doc: 8 (over y, core), ctx: 64 (over x, z).
Axes of the slice: x: 4, y: 4, z: 16, core: 2. Of those that a mesh axis runs over, the one named last changes fastest.
Arguments:
- ctx_query: bfloat16 [131072, 2048], P(('doc', 'ctx')), parts along dimension 0, may hold values from -6 to 6
- ctx_key: bfloat16 [131072, 512], P(('doc', 'ctx')), parts along dimension 0, may hold values from -256 to 256
- ctx_value: bfloat16 [131072, 512], P(('doc', 'ctx')), parts along dimension 0, may hold values from -6 to 6
- step_embed: bfloat16 [32, 4096], P('doc', 'ctx'), parts along dimension 0, may hold values from -6 to 6
- w_query: bfloat16 [4096, 2048], P('ctx'), may hold values from -1 to 1
- w_key: bfloat16 [4096, 512], P('ctx'), may hold values from -4 to 4
- w_value: bfloat16 [4096, 512], P('ctx'), may hold values from -0.09375 to 0.09375
Outputs:
- context_out: bfloat16 [131072, 2048], P(('doc', 'ctx')), parts along dimension 0
- decoded: bfloat16 [32, 2048], P('doc'), parts along dimension 0
There are 8 independent parts, one for each index of `doc`. A program takes and returns all parts, laid end to end along the dimension named above; an argument that names none is the same for every part. Nothing has to cross between parts.
All inputs are finite; a program needn't handle non-finite values.
Results may differ from a plain program's by a relative error of at most 0.008.
The roundings to bfloat16 on the way count: a program that leaves them out, or rounds other values in their place, can miss the bound.
Values may be sent and summed in bfloat16 or wider, within the bound.
No kernel may reach another device: no remote copies, remote signals or barrier semaphores. Data moves between devices by JAX's collectives and lax.ppermute only.
A program may use at most 64 MiB of HBM per device.

v0:
```python
import math

import jax
import jax.numpy as jnp
from jax import lax
from jax.sharding import PartitionSpec as P

HS = 128
HQ = 16
HK = 4
GROUP = 4


def from_root(value, axis, source):
    kept = jnp.where(lax.axis_index(axis) == source, value, 0).astype(value.dtype)
    return lax.psum(kept, axis)


def rotate(values, positions):
    half_width = values.shape[-1] // 2
    frequency = jnp.exp(
        jnp.arange(half_width, dtype=jnp.float32) * (-2.0 * math.log(500000.0) / values.shape[-1])
    )
    angles = positions[:, None] * frequency[None, :]
    cosine = jnp.cos(angles)[:, None, :]
    sine = jnp.sin(angles)[:, None, :]
    first_half = values[..., :half_width]
    second_half = values[..., half_width:]
    return jnp.concatenate(
        [first_half * cosine - second_half * sine, second_half * cosine + first_half * sine],
        axis=-1,
    )


def combine_parts(earlier, later):
    first_max, first_sum, first_out = earlier
    second_max, second_sum, second_out = later
    joint_max = jnp.maximum(first_max, second_max)
    first_factor = jnp.exp(first_max - joint_max)
    second_factor = jnp.exp(second_max - joint_max)
    joint_sum = first_sum * first_factor + second_sum * second_factor
    joint_out = first_out * first_factor[..., None] + second_out * second_factor[..., None]
    return (joint_max, joint_sum, joint_out)


def on_device(ctx_query, ctx_key, ctx_value, step_embed, w_query, w_key, w_value):
    block_len = ctx_query.shape[0]
    step_count = step_embed.shape[0]
    shard_count = lax.axis_size("ctx")
    my_index = lax.axis_index("ctx")
    score_scale = 1.0 / math.sqrt(HS)
    query_part = jnp.dot(step_embed, w_query, preferred_element_type=jnp.float32)
    key_part = jnp.dot(step_embed, w_key, preferred_element_type=jnp.float32)
    value_part = jnp.dot(step_embed, w_value, preferred_element_type=jnp.float32)
    query_sum, key_sum, value_sum = lax.psum((query_part, key_part, value_part), "ctx")
    row_index = jnp.arange(block_len)
    causal = row_index[:, None] >= row_index[None, :]
    use_anchor = my_index != 0
    anchor_pair = from_root(jnp.stack([ctx_key, ctx_value]), "ctx", 0)
    head_outputs = []
    for kv_head in range(HK):
        key_cols = ctx_key[:, kv_head * HS : (kv_head + 1) * HS]
        value_cols = ctx_value[:, kv_head * HS : (kv_head + 1) * HS]
        head_query = ctx_query[:, kv_head * GROUP * HS : (kv_head + 1) * GROUP * HS].reshape(
            block_len, GROUP, HS
        )
        own_scores = (
            jnp.einsum("igd,jd->gij", head_query, key_cols, preferred_element_type=jnp.float32)
            * score_scale
        )
        own_scores = jnp.where(causal, own_scores, -jnp.inf)
        head_pair = anchor_pair[:, :, kv_head * HS : (kv_head + 1) * HS]
        anchor_scores = (
            jnp.einsum("igd,jd->gij", head_query, head_pair[0], preferred_element_type=jnp.float32)
            * score_scale
        )
        anchor_scores = jnp.where(use_anchor, anchor_scores, -jnp.inf)
        row_max = jnp.maximum(jnp.max(own_scores, axis=-1), jnp.max(anchor_scores, axis=-1))
        own_weights = jnp.exp(own_scores - row_max[..., None])
        anchor_weights = jnp.exp(anchor_scores - row_max[..., None])
        row_sum = jnp.sum(own_weights, axis=-1) + jnp.sum(anchor_weights, axis=-1)
        weighted = jnp.einsum(
            "gij,jd->igd",
            own_weights.astype(jnp.bfloat16),
            value_cols,
            preferred_element_type=jnp.float32,
        )
        weighted = weighted + jnp.einsum(
            "gij,jd->igd",
            anchor_weights.astype(jnp.bfloat16),
            head_pair[1],
            preferred_element_type=jnp.float32,
        )
        normed = weighted / jnp.transpose(row_sum, (1, 0))[..., None]
        head_outputs.append(normed.astype(jnp.bfloat16).reshape(block_len, GROUP * HS))
    context_out = jnp.concatenate(head_outputs, axis=1)
    positions = (shard_count * block_len + jnp.arange(step_count)).astype(jnp.float32)
    query_new = (
        rotate(query_sum.reshape(step_count, HQ, HS), positions)
        .astype(jnp.bfloat16)
        .reshape(step_count, HK, GROUP, HS)
    )
    key_new = rotate(key_sum.reshape(step_count, HK, HS), positions).astype(jnp.bfloat16)
    value_new = value_sum.reshape(step_count, HK, HS).astype(jnp.bfloat16)
    cache_keys = ctx_key.reshape(block_len, HK, HS)
    cache_values = ctx_value.reshape(block_len, HK, HS)
    cache_scores = (
        jnp.einsum("shgd,jhd->shgj", query_new, cache_keys, preferred_element_type=jnp.float32)
        * score_scale
    )
    shard_max = jnp.max(cache_scores, axis=-1)
    cache_weights = jnp.exp(cache_scores - shard_max[..., None])
    shard_sum = jnp.sum(cache_weights, axis=-1)
    shard_out = jnp.einsum(
        "shgj,jhd->shgd",
        cache_weights.astype(jnp.bfloat16),
        cache_values,
        preferred_element_type=jnp.float32,
    )
    new_scores = (
        jnp.einsum("shgd,thd->shgt", query_new, key_new, preferred_element_type=jnp.float32)
        * score_scale
    )
    visible = (
        jnp.arange(step_count)[:, None, None, None] >= jnp.arange(step_count)[None, None, None, :]
    )
    new_scores = jnp.where(visible, new_scores, -jnp.inf)
    new_max = jnp.max(new_scores, axis=-1)
    new_weights = jnp.exp(new_scores - new_max[..., None])
    new_sum = jnp.sum(new_weights, axis=-1)
    new_out = jnp.einsum(
        "shgt,thd->shgd",
        new_weights.astype(jnp.bfloat16),
        value_new,
        preferred_element_type=jnp.float32,
    )
    global_max = lax.pmax(shard_max, "ctx")
    shard_factor = jnp.exp(shard_max - global_max)
    total_sum, total_out = lax.psum(
        (shard_sum * shard_factor, shard_out * shard_factor[..., None]), "ctx"
    )
    cache_part = (global_max, total_sum, total_out)
    final_max, final_sum, final_out = combine_parts(cache_part, (new_max, new_sum, new_out))
    decoded = (final_out / final_sum[..., None]).reshape(step_count, HQ * HS).astype(jnp.bfloat16)
    return (context_out, decoded)


def solution(mesh):
    return jax.shard_map(
        on_device,
        mesh=mesh,
        in_specs=(
            P(("doc", "ctx"), None),
            P(("doc", "ctx"), None),
            P(("doc", "ctx"), None),
            P("doc", "ctx"),
            P("ctx", None),
            P("ctx", None),
            P("ctx", None),
        ),
        out_specs=(P(("doc", "ctx"), None), P("doc", None)),
        check_vma=False,
    )
```

profile of v0, /device:TPU:24, one launch (start us, length us, event | category | flops | bytes accessed | tf_op | source)
XLA Modules:
  0.0 749.3 jit_solution(17600917496719842664)
XLA Ops:
  7.3 2.0 maximum_select_fusion
  10.9 0.8 fusion.106
  13.3 285.9 %psum.43 = f32[4,16,128]{2,1,0:T(8,128)S(1)} all-reduce(f32[4,16,128]{2,1,0:T(8,128)S(1)} %bitcast.249), channel_id=1, replica_groups=mesh['doc'=8,'ctx'=64] {'ctx'}, use_global_device_ids=true, to_apply=%region_17.18 | all-reduce | flops 8192 | bytes 65536 | tf_op jit(solution)/shard_map/psum | solution.py:55
  299.5 1.2 fusion.115
  300.8 140.1 %pmax.7 = f32[4,4,4]{2,0,1:T(4,128)S(1)} all-reduce(f32[4,4,4]{2,0,1:T(4,128)S(1)} %get-tuple-element.45), channel_id=1, replica_groups=mesh['doc'=8,'ctx'=64] {'ctx'}, use_global_device_ids=true, to_apply=%region_19.20 | all-reduce | flops 64 | bytes 512 | tf_op jit(solution)/shard_map/pmax | solution.py:137
  441.4 1.2 fusion.34
  442.5 276.0 %all-reduce = (f32[4,4,4,128]{3,2,0,1:T(4,128)S(1)}, f32[4,4,128]{2,0,1:T(4,128)S(1)}, f32[4,4,4]{2,0,1:T(4,128)S(1)}, bf16[4,512]{1,0:T(4,128)(2,1)S(1)}) all-reduce(f32[4,4,4,128]{3,2,0,1:T(4,128)S(1)} %fusion.34, f32[4,4,128]{2,0,1:T(4,128)S(1)} %convolution_bitcast_fusion.11, ...), channel_id=1, replica_groups=mesh['doc'=8,'ctx'=64] {'ctx'}, use_global_device_ids=true, to_apply=%region_20.21 | all-reduce | flops 12352 | bytes 94720 | tf_op jit(solution)/shard_map/psum | solution.py:139
  719.2 1.1 copy.111
  720.3 0.8 copy.109
  721.8 1.3 fusion.111
  723.0 1.1 fusion.113
  724.2 1.3 fusion.108
  725.5 1.2 convolution_bitcast_fusion
  727.0 1.2 fusion.24
  728.1 0.8 copy.65
  729.0 1.3 fusion.110
  730.3 1.2 convolution_bitcast_fusion.1
  731.8 1.9 fusion.25
  733.7 1.2 copy.64
  734.9 1.3 fusion.112
  736.8 1.2 fusion.26
  738.2 1.1 fusion.114
  740.0 1.2 fusion.27
  741.4 1.1 pad_maximum_fusion
  (75 shorter events, 7.5 us)
Async XLA Ops:
  7.2 5.7 copy-start
  7.2 2.1 copy-start.3
  7.2 717.0 %all-reduce.3.cloned.1.call-start = ((), (), s32[]{:S(2)}) async-start(), calls=%async_computation | async-start | bytes 1048576 | tf_op jit(solution)/shard_map/psum | solution.py:16
  7.2 2.8 copy-start.2
  9.2 1.6 copy-start.10
  11.8 0.7 copy-start.6
  12.0 708.3 %copy-start.5 = (bf16[256,512]{0,1:T(8,128)(2,1)}, bf16[256,512]{0,1:T(8,128)(2,1)S(1)}, u32[]{:S(2)}) copy-start(bf16[256,512]{0,1:T(8,128)(2,1)S(1)} %copy.113) | copy-start | bytes 786436
  12.5 0.7 copy-start.14
  12.5 428.6 %copy-start.12 = (bf16[64,512]{1,0:T(8,128)(2,1)S(1)}, bf16[64,512]{1,0:T(8,128)(2,1)}, u32[]{:S(2)}) copy-start(bf16[64,512]{1,0:T(8,128)(2,1)} %param.12) | copy-start | bytes 196612
  12.5 428.7 %copy-start.13 = (bf16[64,512]{1,0:T(8,128)(2,1)S(1)}, bf16[64,512]{1,0:T(8,128)(2,1)}, u32[]{:S(2)}) copy-start(bf16[64,512]{1,0:T(8,128)(2,1)} %param.13) | copy-start | bytes 196612
  720.3 2.7 copy-start.9
  721.7 1.3 copy-start.7
  733.7 2.5 copy-start.1
  733.7 2.5 copy-start.4
  736.8 1.4 copy-start.8
  740.0 1.4 copy-start.11
Sparse Core Ops, SparseCore 0:
  11.4 273.4 all-reduce.2
where the time goes:
time: 750 us; the launch traced here: 749 us
  blocking collectives  702 us (94%)
  matrix products  19.7 us (3%)
  between operations  14.4 us (2%)
  local copies, waits for them, and re-layouts  8.15 us (1%)
    psum x1, blocking collectives, on_device(): lax.psum((query_part, key_part, value_part), 'ctx')  286 us
    psum x1, blocking collectives, on_device(): lax.psum((shard_sum * shard_factor, shard_out * shard_factor[..., None]),...  276 us
    pmax x1, blocking collectives, on_device(): global_max = lax.pmax(shard_max, 'ctx')  140 us
  transfers between devices with their start and end apart: 1, of which 0 were waited for; matrix products, arithmetic and copies ran while one was open for 2% of the time, Pallas kernels for 0%

commit v1 on v0

v1 whole, which is shorter than its diff:
```python
import functools
import math

import jax
import jax.numpy as jnp
from jax import lax
from jax.experimental import pallas as pl
from jax.experimental.pallas import tpu as pltpu
from jax.sharding import Mesh
from jax.sharding import PartitionSpec as P

HS = 128
HQ = 16
HK = 4
GROUP = 4
STEPS = 4
QROWS = GROUP * STEPS
PROWS = QROWS + 2 * STEPS
SCALE = 1.0 / math.sqrt(HS)
EXP2_SCALE = SCALE * math.log2(math.e)
BF16 = jnp.bfloat16
F32 = jnp.float32
INTERPRET = False


def dot(a, b):
    return lax.dot_general(a, b, (((1,), (0,)), ((), ())), preferred_element_type=F32)


def dot_t(a, b):
    return lax.dot_general(a, b, (((1,), (1,)), ((), ())), preferred_element_type=F32)


def split2(value):
    high = value.astype(BF16)
    return high, (value - high.astype(F32)).astype(BF16)


def split3(value):
    high = value.astype(BF16)
    rest = value - high.astype(F32)
    middle = rest.astype(BF16)
    return high, middle, (rest - middle.astype(F32)).astype(BF16)


def project_kernel(embed_ref, wq_ref, wk_ref, wv_ref, key_ref, value_ref, out_ref):
    block = key_ref.shape[0]
    pick = (
        lax.broadcasted_iota(jnp.int32, (PROWS, STEPS), 0) % STEPS
        == lax.broadcasted_iota(jnp.int32, (PROWS, STEPS), 1)
    )
    repeated = dot(pick.astype(BF16), embed_ref[...]).astype(BF16)
    row_head = lax.broadcasted_iota(jnp.int32, repeated.shape, 0) // STEPS
    placed = [jnp.where(row_head == j, repeated, 0).astype(BF16) for j in range(GROUP + 2)]
    for group in range(HK):
        cols = slice(group * HS, (group + 1) * HS)
        part = dot(placed[GROUP], wk_ref[:, cols]) + dot(placed[GROUP + 1], wv_ref[:, cols])
        for j in range(GROUP):
            head = group * GROUP + j
            part = part + dot(placed[j], wq_ref[:, head * HS : (head + 1) * HS])
        high, low = split2(part)
        out_ref[group, 0:PROWS] = high
        out_ref[group, PROWS : 2 * PROWS] = low
        out_ref[group, 2 * PROWS : 2 * PROWS + block] = key_ref[:, cols]
        out_ref[group, 2 * PROWS + block : 2 * PROWS + 2 * block] = value_ref[:, cols]


def spread_kernel(in_ref, out_ref):
    sources = in_ref.shape[0]
    peers = out_ref.shape[0]
    piece = (in_ref.shape[1] - 2 * PROWS) // peers
    total = in_ref[0, 0:PROWS].astype(F32) + in_ref[0, PROWS : 2 * PROWS].astype(F32)
    for source in range(1, sources):
        total = total + (
            in_ref[source, 0:PROWS].astype(F32) + in_ref[source, PROWS : 2 * PROWS].astype(F32)
        )
    high, low = split2(total)
    for peer in range(peers):
        out_ref[peer, 0:PROWS] = high
        out_ref[peer, PROWS : 2 * PROWS] = low
        start = 2 * PROWS + peer * piece
        out_ref[peer, 2 * PROWS : 2 * PROWS + piece] = in_ref[0, start : start + piece]


def decode_kernel(sums_ref, cache_ref, cos_ref, sin_ref, out_ref, new_ref):
    peers = sums_ref.shape[0]
    blocks = cache_ref.shape[0]
    block = (cache_ref.shape[1] - 2 * PROWS) // 2
    piece = sums_ref.shape[1] - 2 * PROWS
    total = sums_ref[0, 0:PROWS].astype(F32) + sums_ref[0, PROWS : 2 * PROWS].astype(F32)
    for peer in range(1, peers):
        total = total + (
            sums_ref[peer, 0:PROWS].astype(F32) + sums_ref[peer, PROWS : 2 * PROWS].astype(F32)
        )
    rotated = total * cos_ref[...] + pltpu.roll(total, HS // 2, 1) * sin_ref[...]
    query = rotated[0:QROWS].astype(BF16)
    parts = []
    for c in range(blocks):
        keys = cache_ref[c, 2 * PROWS : 2 * PROWS + block]
        values = cache_ref[c, 2 * PROWS + block : 2 * PROWS + 2 * block]
        scores = dot_t(query, keys) * SCALE
        part_max = jnp.max(scores, axis=1, keepdims=True)
        weights = jnp.exp(scores - part_max)
        part_sum = jnp.sum(weights, axis=1, keepdims=True)
        parts.append((part_max, part_sum, dot(weights.astype(BF16), values)))
    joint_max = functools.reduce(jnp.maximum, [part[0] for part in parts])
    joint_sum, joint_out = 0.0, 0.0
    for part_max, part_sum, part_out in parts:
        factor = jnp.exp(part_max - joint_max)
        joint_sum = joint_sum + part_sum * factor
        joint_out = joint_out + part_out * factor
    lane = lax.broadcasted_iota(jnp.int32, (QROWS, HS), 1)
    stats = jnp.zeros((QROWS, HS), F32)
    for at, value in enumerate(split3(joint_max) + split3(joint_sum)):
        stats = jnp.where(lane == at, value.astype(F32), stats)
    stats = stats.astype(BF16)
    high, low = split2(joint_out)
    anchor = sums_ref[0, 2 * PROWS : 2 * PROWS + piece]
    for peer in range(peers):
        out_ref[peer, 0:QROWS] = high
        out_ref[peer, QROWS : 2 * QROWS] = low
        out_ref[peer, 2 * QROWS : 3 * QROWS] = stats
        out_ref[peer, 3 * QROWS : 3 * QROWS + piece] = anchor
    key_new = rotated[QROWS:PROWS].astype(BF16)
    value_new = pltpu.roll(total[QROWS:PROWS], STEPS, 0).astype(BF16)
    scores = dot_t(query, key_new) * SCALE
    step = lax.broadcasted_iota(jnp.int32, scores.shape, 0) % STEPS
    later = lax.broadcasted_iota(jnp.int32, scores.shape, 1)
    scores = jnp.where(later <= step, scores, -jnp.inf)
    new_max = jnp.max(scores, axis=1, keepdims=True)
    weights = jnp.exp(scores - new_max)
    new_sum = jnp.sum(weights, axis=1, keepdims=True)
    new_ref[0] = jnp.broadcast_to(new_max, (QROWS, HS))
    new_ref[1] = jnp.broadcast_to(new_sum, (QROWS, HS))
    new_ref[2] = dot(weights.astype(BF16), value_new)


def combine_kernel(parts_ref, new_ref, out_ref):
    peers = parts_ref.shape[0]
    piece = parts_ref.shape[1] - 3 * QROWS
    maxima, sums, outs = [], [], []
    for peer in range(peers):
        stats = parts_ref[peer, 2 * QROWS : 3 * QROWS].astype(F32)
        maxima.append(stats[:, 0:1] + stats[:, 1:2] + stats[:, 2:3])
        sums.append(stats[:, 3:4] + stats[:, 4:5] + stats[:, 5:6])
    new_max = new_ref[0][:, 0:1]
    global_max = functools.reduce(jnp.maximum, maxima + [new_max])
    factor = jnp.exp(new_max - global_max)
    total_sum = new_ref[1][:, 0:1] * factor
    total_out = new_ref[2] * factor
    for peer in range(peers):
        factor = jnp.exp(maxima[peer] - global_max)
        part_out = parts_ref[peer, 0:QROWS].astype(F32) + parts_ref[peer, QROWS : 2 * QROWS].astype(F32)
        total_sum = total_sum + sums[peer] * factor
        total_out = total_out + part_out * factor
    decoded = (total_out / total_sum).astype(BF16)
    for x in range(out_ref.shape[0]):
        out_ref[x, 0:QROWS] = decoded
        for peer in range(peers):
            start = QROWS + peer * piece
            out_ref[x, start : start + piece] = parts_ref[peer, 3 * QROWS : 3 * QROWS + piece]


def prefill_kernel(query_ref, key_ref, value_ref, anchor_ref, out_ref, decoded_ref):
    block = key_ref.shape[0]
    half = block // 2
    use_anchor = (lax.axis_index("x") + lax.axis_index("z")) != 0
    anchor_key = anchor_ref[0, QROWS : QROWS + block]
    anchor_value = anchor_ref[0, QROWS + block : QROWS + 2 * block]
    causal = lax.broadcasted_iota(jnp.int32, (half, half), 0) >= lax.broadcasted_iota(
        jnp.int32, (half, half), 1
    )
    for j in range(GROUP):
        cols = slice(j * HS, (j + 1) * HS)
        for part in range(2):
            rows = slice(part * half, (part + 1) * half)
            seen = (part + 1) * half
            query = query_ref[rows, cols]
            own = dot_t(query, key_ref[0:seen, :])
            diagonal = jnp.where(causal, own[:, part * half :], -jnp.inf)
            own = diagonal if part == 0 else jnp.concatenate([own[:, :half], diagonal], axis=1)
            anchor = dot_t(query, anchor_key)
            own_max = jnp.max(own, axis=1, keepdims=True)
            anchor_max = jnp.max(anchor, axis=1, keepdims=True)
            row_max = jnp.where(use_anchor, jnp.maximum(own_max, anchor_max), own_max)
            own_weights = jnp.exp2((own - row_max) * EXP2_SCALE)
            anchor_shift = jnp.where(use_anchor, row_max, jnp.inf)
            anchor_weights = jnp.exp2((anchor - anchor_shift) * EXP2_SCALE)
            row_sum = jnp.sum(own_weights, axis=1, keepdims=True) + jnp.sum(
                anchor_weights, axis=1, keepdims=True
            )
            weighted = dot(own_weights.astype(BF16), value_ref[0:seen, :]) + dot(
                anchor_weights.astype(BF16), anchor_value
            )
            out_ref[rows, cols] = (weighted / row_sum).astype(BF16)
        pick = (
            lax.broadcasted_iota(jnp.int32, (STEPS, QROWS), 1)
            == lax.broadcasted_iota(jnp.int32, (STEPS, QROWS), 0) + j * STEPS
        )
        decoded_ref[:, cols] = dot(pick.astype(BF16), anchor_ref[0, 0:QROWS]).astype(BF16)


def rotary_tables(position, step_count):
    half_width = HS // 2
    frequency = jnp.exp(
        jnp.arange(half_width, dtype=F32) * (-2.0 * math.log(500000.0) / HS)
    )
    positions = (position + jnp.arange(step_count)).astype(F32)
    angles = positions[:, None] * frequency[None, :]
    cosine, sine = jnp.cos(angles), jnp.sin(angles)
    cosine = jnp.concatenate([cosine, cosine], axis=1)
    sine = jnp.concatenate([-sine, sine], axis=1)
    return jnp.tile(cosine, (GROUP + 2, 1)), jnp.tile(sine, (GROUP + 2, 1))


def call(kernel, out_shape, **kwargs):
    return pl.pallas_call(kernel, out_shape=out_shape, interpret=INTERPRET, **kwargs)


def on_device(ctx_query, ctx_key, ctx_value, step_embed, w_query, w_key, w_value):
    block = ctx_query.shape[0]
    nx, nz = lax.axis_size("x"), lax.axis_size("z")
    piece = 2 * block // nz
    shape = jax.ShapeDtypeStruct
    cosine, sine = rotary_tables(nx * nz * block, STEPS)

    slabs = call(project_kernel, shape((nx, 2 * PROWS + 2 * block, HS), BF16), name="project")(
        step_embed, w_query, w_key, w_value, ctx_key, ctx_value
    )
    cache = lax.all_to_all(slabs, "x", 0, 0, tiled=True)
    spread = call(spread_kernel, shape((nz, 2 * PROWS + piece, HS), BF16), name="spread")(cache)
    sums = lax.all_to_all(spread, "z", 0, 0, tiled=True)
    parts, new = call(
        decode_kernel,
        (shape((nz, 3 * QROWS + piece, HS), BF16), shape((3, QROWS, HS), F32)),
        name="decode",
    )(sums, cache, cosine, sine)
    parts = lax.all_to_all(parts, "z", 0, 0, tiled=True)
    heads = call(combine_kernel, shape((nx, QROWS + 2 * block, HS), BF16), name="combine")(parts, new)
    heads = lax.all_to_all(heads, "x", 0, 0, tiled=True)
    width = GROUP * HS
    context_out, decoded = call(
        prefill_kernel,
        (shape((block, HQ * HS), BF16), shape((STEPS, HQ * HS), BF16)),
        name="prefill",
        grid=(HK,),
        in_specs=[
            pl.BlockSpec((block, width), lambda h: (0, h)),
            pl.BlockSpec((block, HS), lambda h: (0, h)),
            pl.BlockSpec((block, HS), lambda h: (0, h)),
            pl.BlockSpec((1, QROWS + 2 * block, HS), lambda h: (h, 0, 0)),
        ],
        out_specs=[
            pl.BlockSpec((block, width), lambda h: (0, h)),
            pl.BlockSpec((STEPS, width), lambda h: (0, h)),
        ],
    )(ctx_query, ctx_key, ctx_value, heads)
    return context_out, decoded


def solution(mesh):
    docs, contexts = mesh.shape["doc"], mesh.shape["ctx"]
    split = Mesh(mesh.devices.reshape(docs, HK, contexts // HK), ("doc", "x", "z"))
    ctx = ("x", "z")
    rows = P(("doc",) + ctx, None)
    return jax.shard_map(
        on_device,
        mesh=split,
        in_specs=(rows, rows, rows, P("doc", ctx), P(ctx, None), P(ctx, None), P(ctx, None)),
        out_specs=(rows, P("doc", None)),
        check_vma=False,
    )
```

time: 750 us -> 111 us (0.15)
  blocking collectives: 702 us -> 53.2 us
  Pallas kernels: 0 us -> 20.6 us
  matrix products: 19.7 us -> 0 us
  waiting for transfers between devices: 0.04 us -> 19.6 us
  starting transfers between devices: 0.04 us -> 15.2 us
  between operations: 14.4 us -> 0.66 us
    psum x2 -> x0, blocking collectives: 562 us -> none  [the longest x1 286 us: on_device(): lax.psum((query_part, key_part, value_part), 'ctx')]
    pmax x1 -> x0, blocking collectives: 140 us -> none  [on_device(): global_max = lax.pmax(shard_max, 'ctx')]
    all_to_all x0 -> x3, blocking collectives: none -> 53.2 us  [the longest x1 26.4 us: on_device(): parts = lax.all_to_all(parts, 'z', 0, 0, tiled=True)]
    pallas_call x0 -> x5, Pallas kernels: none -> 20.6 us  [the longest x1 11.2 us: on_device(): call(prefill_kernel, (shape((block, HQ * HS), BF16), shape((STEPS, HQ * H...]
    dot_general x23 -> x0, matrix products: 19.7 us -> none  [the longest x4 5.46 us: on_device(): jnp.einsum('gij,jd->igd', anchor_weights.astype(jnp.bfloat16), head_pair[...]
    all_to_all x0 -> x1, waiting for transfers between devices: none -> 19.6 us  [on_device(): sums = lax.all_to_all(spread, 'z', 0, 0, tiled=True)]
    all_to_all x0 -> x1, starting transfers between devices: none -> 15.2 us  [on_device(): sums = lax.all_to_all(spread, 'z', 0, 0, tiled=True)]
  transfers between devices with their start and end apart: 1 -> 1, of which waited for: 0 -> 1; matrix products, arithmetic and copies ran while one was open for 2% -> 0% of each run, Pallas kernels for 0% -> 0%
where the time goes in v1:
time: 111 us
  blocking collectives  53.2 us (48%)
  Pallas kernels  20.6 us (19%)
  waiting for transfers between devices  19.6 us (18%)
  starting transfers between devices  15.2 us (14%)
  local copies, waits for them, and re-layouts  1.25 us (1%)
    all_to_all x1, blocking collectives, on_device(): parts = lax.all_to_all(parts, 'z', 0, 0, tiled=True)  26.4 us
    all_to_all x1, waiting for transfers between devices, on_device(): sums = lax.all_to_all(spread, 'z', 0, 0, tiled=True)  19.6 us
    all_to_all x1, starting transfers between devices, on_device(): sums = lax.all_to_all(spread, 'z', 0, 0, tiled=True)  15.2 us
    all_to_all x1, blocking collectives, on_device(): cache = lax.all_to_all(slabs, 'x', 0, 0, tiled=True)  14.5 us
    all_to_all x1, blocking collectives, on_device(): heads = lax.all_to_all(heads, 'x', 0, 0, tiled=True)  12.4 us
    pallas_call x1, Pallas kernels, on_device(): call(prefill_kernel, (shape((block, HQ * HS), BF16), shape((STEPS, HQ * H...  11.2 us
    pallas_call x1, Pallas kernels, on_device(): call(decode_kernel, (shape((nz, 3 * QROWS + piece, HS), BF16), shape((3,...  3.12 us
    pallas_call x1, Pallas kernels, on_device(): call(project_kernel, shape((nx, 2 * PROWS + 2 * block, HS), BF16), name='...  2.34 us
  transfers between devices with their start and end apart: 1, of which 1 were waited for; matrix products, arithmetic and copies ran while one was open for 0% of the time, Pallas kernels for 0%

profile of v1, /device:TPU:24, one launch (start us, length us, event | category | flops | bytes accessed | tf_op | source)
XLA Modules:
  0.0 110.7 jit_solution(6613403041104474765)
XLA Ops:
  0.6 2.3 %project.1 = bf16[4,560,128]{2,1,0:T(8,128)(2,1)} custom-call(bf16[4,64]{1,0:T(4,128)(2,1)} %embed_ref.1, bf16[64,2048]{1,0:T(8,128)(2,1)} %wq_ref.1, bf16[64,512]{1,0:T(8,128)(2,1)} %wk_ref.1, bf16[64,512]{1,0:T(8,128)(2,1)} %wv_ref.1, bf16[256,512]{1,0:T(8,128)(2,1)} %key_ref.3, bf16[256,512]{1,0:T(8,128)(2,1)} %value_ref.3), custom_call_target="tpu_custom_call" | custom-call | tf_op jit(solution)/shard_map/project/pallas_call | solution.py:227
  3.0 14.5 %all_to_all.20.in_ref.cache_ref = bf16[4,560,128]{2,1,0:T(8,128)(2,1)} all-to-all(bf16[4,560,128]{2,1,0:T(8,128)(2,1)} %project.1), channel_id=1, replica_groups=mesh['doc'=8,'x'=4,'z'=16] {'x'}, dimensions={0} | all-to-all | bytes 1146880 | tf_op jit(solution)/shard_map/all_to_all | solution.py:230
  17.5 1.8 %spread.1 = bf16[16,80,128]{2,1,0:T(8,128)(2,1)} custom-call(bf16[4,560,128]{2,1,0:T(8,128)(2,1)} %all_to_all.20.in_ref.cache_ref), custom_call_target="tpu_custom_call" | custom-call | tf_op jit(solution)/shard_map/spread/pallas_call | solution.py:231
  19.3 15.2 %all-to-all-start.1 = ((bf16[16,80,128]{2,1,0:T(8,128)(2,1)}), bf16[16,80,128]{2,1,0:T(8,128)(2,1)S(1)}, u32[]{:S(2)}, u32[]{:S(2)}) async-start(bf16[16,80,128]{2,1,0:T(8,128)(2,1)} %spread.1), calls=%async_computation.1 | async-start | bytes 655360 | tf_op jit(solution)/shard_map/all_to_all | solution.py:232
  34.5 0.1 fusion
  34.6 0.1 pad_maximum_fusion
  34.7 19.6 %all-to-all-done.1.sums_ref = bf16[16,80,128]{2,1,0:T(8,128)(2,1)S(1)} async-done(((bf16[16,80,128]{2,1,0:T(8,128)(2,1)}), bf16[16,80,128]{2,1,0:T(8,128)(2,1)S(1)}, u32[]{:S(2)}, u32[]{:S(2)}) %all-to-all-start.1) | async-done | bytes 327712 | tf_op jit(solution)/shard_map/all_to_all | solution.py:232
  54.3 0.0 copy-start
  54.3 0.6 tile.8
  54.9 0.6 tile.20
  55.5 0.0 copy-done
  55.5 3.1 %decode.1 = (bf16[16,80,128]{2,1,0:T(8,128)(2,1)}, f32[3,16,128]{2,1,0:T(8,128)}) custom-call(bf16[16,80,128]{2,1,0:T(8,128)(2,1)} %copy-done, bf16[4,560,128]{2,1,0:T(8,128)(2,1)} %all_to_all.20.in_ref.cache_ref, f32[24,128]{1,0:T(8,128)} %bitcast.2, f32[24,128]{1,0:T(8,128)} %bitcast.3), custom_call_target="tpu_custom_call" | custom-call | tf_op jit(solution)/shard_map/decode/pallas_call | solution.py:233
  58.6 26.4 %all_to_all.21.parts_ref = bf16[16,80,128]{2,1,0:T(8,128)(2,1)} all-to-all(bf16[16,80,128]{2,1,0:T(8,128)(2,1)} %get-tuple-element.4), channel_id=1, replica_groups=mesh['doc'=8,'x'=4,'z'=16] {'z'}, dimensions={0} | all-to-all | bytes 655360 | tf_op jit(solution)/shard_map/all_to_all | solution.py:238
  85.0 2.1 %combine.1 = bf16[4,528,128]{2,1,0:T(8,128)(2,1)} custom-call(bf16[16,80,128]{2,1,0:T(8,128)(2,1)} %all_to_all.21.parts_ref, f32[3,16,128]{2,1,0:T(8,128)} %get-tuple-element.5.new_ref), custom_call_target="tpu_custom_call" | custom-call | tf_op jit(solution)/shard_map/combine/pallas_call | solution.py:239
  87.1 12.4 %all_to_all.22.anchor_ref = bf16[4,528,128]{2,1,0:T(8,128)(2,1)} all-to-all(bf16[4,528,128]{2,1,0:T(8,128)(2,1)} %combine.1), channel_id=1, replica_groups=mesh['doc'=8,'x'=4,'z'=16] {'x'}, dimensions={0} | all-to-all | bytes 1081344 | tf_op jit(solution)/shard_map/all_to_all | solution.py:240
  99.5 11.2 %prefill.1 = (bf16[256,2048]{1,0:T(8,128)(2,1)}, bf16[4,2048]{1,0:T(4,128)(2,1)}) custom-call(bf16[256,2048]{1,0:T(8,128)(2,1)} %query_ref.1, bf16[256,512]{1,0:T(8,128)(2,1)} %key_ref.3, bf16[256,512]{1,0:T(8,128)(2,1)} %value_ref.3, bf16[4,528,128]{2,1,0:T(8,128)(2,1)} %all_to_all.22.anchor_ref), custom_call_target="tpu_custom_call" | custom-call | tf_op jit(solution)/shard_map/prefill/pallas_call | solution.py:242
  (2 shorter events, 0.0 us)
Async XLA Ops:
  19.3 35.0 %all-to-all-start.1 = ((bf16[16,80,128]{2,1,0:T(8,128)(2,1)}), bf16[16,80,128]{2,1,0:T(8,128)(2,1)S(1)}, u32[]{:S(2)}, u32[]{:S(2)}) async-start(bf16[16,80,128]{2,1,0:T(8,128)(2,1)} %spread.1), calls=%async_computation.1 | async-start | bytes 655360 | tf_op jit(solution)/shard_map/all_to_all | solution.py:232
  54.3 1.2 %copy-start = (bf16[16,80,128]{2,1,0:T(8,128)(2,1)}, bf16[16,80,128]{2,1,0:T(8,128)(2,1)S(1)}, u32[]{:S(2)}) copy-start(bf16[16,80,128]{2,1,0:T(8,128)(2,1)S(1)} %all-to-all-done.1.sums_ref) | copy-start | bytes 983044

commit v2 on v1

v2 whole, which is shorter than its diff:
```python
import functools
import math

import jax
import jax.numpy as jnp
from jax import lax
from jax.experimental import pallas as pl
from jax.experimental.pallas import tpu as pltpu
from jax.sharding import Mesh
from jax.sharding import PartitionSpec as P

HS = 128
HQ = 16
HK = 4
GROUP = 4
STEPS = 4
QROWS = GROUP * STEPS
PROWS = QROWS + 2 * STEPS
SROWS = QROWS // 2
SCALE = 1.0 / math.sqrt(HS)
EXP2_SCALE = SCALE * math.log2(math.e)
BF16 = jnp.bfloat16
F32 = jnp.float32
INTERPRET = False


def dot(a, b):
    return lax.dot_general(a, b, (((1,), (0,)), ((), ())), preferred_element_type=F32)


def dot_t(a, b):
    return lax.dot_general(a, b, (((1,), (1,)), ((), ())), preferred_element_type=F32)


def split2(value):
    high = value.astype(BF16)
    return high, (value - high.astype(F32)).astype(BF16)


def split3(value):
    high = value.astype(BF16)
    rest = value - high.astype(F32)
    middle = rest.astype(BF16)
    return high, middle, (rest - middle.astype(F32)).astype(BF16)


def project_kernel(embed_ref, wq_ref, wk_ref, wv_ref, key_ref, value_ref, out_ref, part_ref):
    block = key_ref.shape[0]
    embed = embed_ref[...]
    query, key, value = dot(embed, wq_ref[...]), dot(embed, wk_ref[...]), dot(embed, wv_ref[...])
    for group in range(HK):
        cols = slice(group * HS, (group + 1) * HS)
        for j in range(GROUP):
            head = group * GROUP + j
            part_ref[group, j * STEPS : (j + 1) * STEPS] = query[:, head * HS : (head + 1) * HS]
        part_ref[group, QROWS : QROWS + STEPS] = key[:, cols]
        part_ref[group, QROWS + STEPS : PROWS] = value[:, cols]
        out_ref[group, 2 * PROWS : 2 * PROWS + block] = key_ref[:, cols]
        out_ref[group, 2 * PROWS + block : 2 * PROWS + 2 * block] = value_ref[:, cols]
    for group in range(HK):
        high, low = split2(part_ref[group])
        out_ref[group, 0:PROWS] = high
        out_ref[group, PROWS : 2 * PROWS] = low


def spread_kernel(in_ref, out_ref):
    sources = in_ref.shape[0]
    peers = out_ref.shape[0]
    piece = (in_ref.shape[1] - 2 * PROWS) // peers
    total = in_ref[0, 0:PROWS].astype(F32) + in_ref[0, PROWS : 2 * PROWS].astype(F32)
    for source in range(1, sources):
        total = total + (
            in_ref[source, 0:PROWS].astype(F32) + in_ref[source, PROWS : 2 * PROWS].astype(F32)
        )
    high, low = split2(total)
    for peer in range(peers):
        out_ref[peer, 0:PROWS] = high
        out_ref[peer, PROWS : 2 * PROWS] = low
        start = 2 * PROWS + peer * piece
        out_ref[peer, 2 * PROWS : 2 * PROWS + piece] = in_ref[0, start : start + piece]


def decode_kernel(sums_ref, cache_ref, cos_ref, sin_ref, out_ref, new_ref):
    peers = sums_ref.shape[0]
    blocks = cache_ref.shape[0]
    block = (cache_ref.shape[1] - 2 * PROWS) // 2
    piece = sums_ref.shape[1] - 2 * PROWS
    total = sums_ref[0, 0:PROWS].astype(F32) + sums_ref[0, PROWS : 2 * PROWS].astype(F32)
    for peer in range(1, peers):
        total = total + (
            sums_ref[peer, 0:PROWS].astype(F32) + sums_ref[peer, PROWS : 2 * PROWS].astype(F32)
        )
    rotated = total * cos_ref[...] + pltpu.roll(total, HS // 2, 1) * sin_ref[...]
    query = rotated[0:QROWS].astype(BF16)
    parts = []
    for c in range(blocks):
        keys = cache_ref[c, 2 * PROWS : 2 * PROWS + block]
        values = cache_ref[c, 2 * PROWS + block : 2 * PROWS + 2 * block]
        scores = dot_t(query, keys) * SCALE
        part_max = jnp.max(scores, axis=1, keepdims=True)
        weights = jnp.exp(scores - part_max)
        part_sum = jnp.sum(weights, axis=1, keepdims=True)
        parts.append((part_max, part_sum, dot(weights.astype(BF16), values)))
    joint_max = functools.reduce(jnp.maximum, [part[0] for part in parts])
    joint_sum, joint_out = 0.0, 0.0
    for part_max, part_sum, part_out in parts:
        factor = jnp.exp(part_max - joint_max)
        joint_sum = joint_sum + part_sum * factor
        joint_out = joint_out + part_out * factor
    lane = lax.broadcasted_iota(jnp.int32, (QROWS, HS), 1)
    stats = jnp.zeros((QROWS, HS), F32)
    for at, value in enumerate(split3(joint_max) + split3(joint_sum)):
        stats = jnp.where(lane == at, value.astype(F32), stats)
    stats = jnp.where(lane[:SROWS] < HS // 2, stats[:SROWS], pltpu.roll(stats[SROWS:], HS // 2, 1))
    stats = stats.astype(BF16)
    joint_out = joint_out.astype(BF16)
    anchor = sums_ref[0, 2 * PROWS : 2 * PROWS + piece]
    for peer in range(peers):
        out_ref[peer, 0:QROWS] = joint_out
        out_ref[peer, QROWS : QROWS + SROWS] = stats
        out_ref[peer, QROWS + SROWS : QROWS + SROWS + piece] = anchor
    key_new = rotated[QROWS:PROWS].astype(BF16)
    value_new = pltpu.roll(total[QROWS:PROWS], STEPS, 0).astype(BF16)
    scores = dot_t(query, key_new) * SCALE
    step = lax.broadcasted_iota(jnp.int32, scores.shape, 0) % STEPS
    later = lax.broadcasted_iota(jnp.int32, scores.shape, 1)
    scores = jnp.where(later <= step, scores, -jnp.inf)
    new_max = jnp.max(scores, axis=1, keepdims=True)
    weights = jnp.exp(scores - new_max)
    new_sum = jnp.sum(weights, axis=1, keepdims=True)
    new_ref[0] = jnp.broadcast_to(new_max, (QROWS, HS))
    new_ref[1] = jnp.broadcast_to(new_sum, (QROWS, HS))
    new_ref[2] = dot(weights.astype(BF16), value_new)


def combine_kernel(parts_ref, new_ref, out_ref):
    peers = parts_ref.shape[0]
    first = QROWS + SROWS
    piece = parts_ref.shape[1] - first
    maxima, sums = [], []
    for peer in range(peers):
        stats = parts_ref[peer, QROWS:first].astype(F32)
        stats = jnp.concatenate([stats, pltpu.roll(stats, HS // 2, 1)], axis=0)
        maxima.append(stats[:, 0:1] + stats[:, 1:2] + stats[:, 2:3])
        sums.append(stats[:, 3:4] + stats[:, 4:5] + stats[:, 5:6])
    new_max = new_ref[0][:, 0:1]
    global_max = functools.reduce(jnp.maximum, maxima + [new_max])
    factor = jnp.exp(new_max - global_max)
    total_sum = new_ref[1][:, 0:1] * factor
    total_out = new_ref[2] * factor
    for peer in range(peers):
        factor = jnp.exp(maxima[peer] - global_max)
        total_sum = total_sum + sums[peer] * factor
        total_out = total_out + parts_ref[peer, 0:QROWS].astype(F32) * factor
    decoded = (total_out / total_sum).astype(BF16)
    for x in range(out_ref.shape[0]):
        out_ref[x, 0:QROWS] = decoded
        for peer in range(peers):
            start = QROWS + peer * piece
            out_ref[x, start : start + piece] = parts_ref[peer, first : first + piece]


def prefill_kernel(query_ref, key_ref, value_ref, anchor_ref, out_ref, decoded_ref):
    block = key_ref.shape[0]
    half = block // 2
    group = pl.program_id(0)
    use_anchor = (lax.axis_index("x") + lax.axis_index("z")) != 0
    head_cols = pl.ds(pl.multiple_of(group * HS, HS), HS)
    key = key_ref[:, head_cols]
    anchor_key = anchor_ref[group, QROWS : QROWS + block]
    anchor_value = anchor_ref[group, QROWS + block : QROWS + 2 * block]
    values = jnp.concatenate([anchor_value.T, value_ref[:, head_cols].T], axis=1)
    causal = lax.broadcasted_iota(jnp.int32, (half, half), 0) <= lax.broadcasted_iota(
        jnp.int32, (half, half), 1
    )
    for j in range(GROUP):
        cols = slice(j * HS, (j + 1) * HS)
        query = query_ref[:, pl.ds(pl.multiple_of((group * GROUP + j) * HS, HS), HS)]
        anchor_scores = dot_t(anchor_key, query)
        early_scores = dot_t(key[:half], query)
        late_scores = dot_t(key[half:], query[half:])
        for part in range(2):
            rows = slice(part * half, (part + 1) * half)
            anchor = anchor_scores[:, rows]
            if part == 0:
                own = jnp.where(causal, early_scores[:, rows], -jnp.inf)
            else:
                own = jnp.concatenate(
                    [early_scores[:, rows], jnp.where(causal, late_scores, -jnp.inf)], axis=0
                )
            own_max = jnp.max(own, axis=0, keepdims=True)
            anchor_max = jnp.max(anchor, axis=0, keepdims=True)
            row_max = jnp.where(use_anchor, jnp.maximum(own_max, anchor_max), own_max)
            anchor_shift = jnp.where(use_anchor, row_max, jnp.inf)
            own_weights = jnp.exp2((own - row_max) * EXP2_SCALE)
            anchor_weights = jnp.exp2((anchor - anchor_shift) * EXP2_SCALE)
            row_sum = jnp.sum(own_weights, axis=0, keepdims=True) + jnp.sum(
                anchor_weights, axis=0, keepdims=True
            )
            weights = jnp.concatenate(
                [anchor_weights.astype(BF16), own_weights.astype(BF16)], axis=0
            )
            weighted = dot(values[:, : block + (part + 1) * half], weights)
            out_ref[rows, cols] = (weighted * (1.0 / row_sum)).T.astype(BF16)
        pick = (
            lax.broadcasted_iota(jnp.int32, (STEPS, QROWS), 1)
            == lax.broadcasted_iota(jnp.int32, (STEPS, QROWS), 0) + j * STEPS
        )
        decoded_ref[:, cols] = dot(pick.astype(BF16), anchor_ref[group, 0:QROWS]).astype(BF16)


def rotary_tables(position):
    shape = (PROWS, HS)
    lane = lax.broadcasted_iota(jnp.int32, shape, 1)
    step = lax.broadcasted_iota(jnp.int32, shape, 0) % STEPS
    half_width = HS // 2
    frequency = jnp.exp((lane % half_width).astype(F32) * (-2.0 * math.log(500000.0) / HS))
    angles = (position + step).astype(F32) * frequency
    sine = jnp.sin(angles)
    return jnp.cos(angles), jnp.where(lane < half_width, -sine, sine)


VMEM_SPEC = pl.BlockSpec(memory_space=pltpu.VMEM)


def in_vmem(value):
    return value if INTERPRET else pltpu.with_memory_space_constraint(value, pltpu.VMEM)


def call(kernel, out_shape, **kwargs):
    if not INTERPRET:
        out_shape = jax.tree.map(lambda out: pltpu.VMEM(out.shape, out.dtype), out_shape)
    return pl.pallas_call(
        kernel,
        out_shape=out_shape,
        out_specs=jax.tree.map(lambda _: VMEM_SPEC, out_shape),
        interpret=INTERPRET,
        **kwargs,
    )


def on_device(ctx_query, ctx_key, ctx_value, step_embed, w_query, w_key, w_value):
    block = ctx_query.shape[0]
    nx, nz = lax.axis_size("x"), lax.axis_size("z")
    piece = 2 * block // nz
    shape = jax.ShapeDtypeStruct
    cosine, sine = rotary_tables(nx * nz * block)

    slabs = call(
        project_kernel,
        shape((nx, 2 * PROWS + 2 * block, HS), BF16),
        name="project",
        scratch_shapes=[pltpu.VMEM((HK, PROWS, HS), F32)],
    )(step_embed, w_query, w_key, w_value, ctx_key, ctx_value)
    cache = in_vmem(lax.all_to_all(slabs, "x", 0, 0, tiled=True))
    spread = call(
        spread_kernel,
        shape((nz, 2 * PROWS + piece, HS), BF16),
        name="spread",
        in_specs=[VMEM_SPEC],
    )(cache)
    sums = in_vmem(lax.all_to_all(spread, "z", 0, 0, tiled=True))
    parts, new = call(
        decode_kernel,
        (shape((nz, QROWS + SROWS + piece, HS), BF16), shape((3, QROWS, HS), F32)),
        name="decode",
        in_specs=[VMEM_SPEC] * 4,
    )(sums, cache, in_vmem(cosine), in_vmem(sine))
    parts = in_vmem(lax.all_to_all(parts, "z", 0, 0, tiled=True))
    heads = call(
        combine_kernel,
        shape((nx, QROWS + 2 * block, HS), BF16),
        name="combine",
        in_specs=[VMEM_SPEC] * 2,
    )(parts, in_vmem(new))
    heads = in_vmem(lax.all_to_all(heads, "x", 0, 0, tiled=True))
    width = GROUP * HS
    context_out, decoded = pl.pallas_call(
        prefill_kernel,
        out_shape=(shape((block, HQ * HS), BF16), shape((STEPS, HQ * HS), BF16)),
        name="prefill",
        grid=(HK,),
        in_specs=[VMEM_SPEC] * 4,
        out_specs=[
            pl.BlockSpec((block, width), lambda h: (0, h)),
            pl.BlockSpec((STEPS, width), lambda h: (0, h)),
        ],
        interpret=INTERPRET,
    )(in_vmem(ctx_query), in_vmem(ctx_key), in_vmem(ctx_value), heads)
    return context_out, decoded


def solution(mesh):
    docs, contexts = mesh.shape["doc"], mesh.shape["ctx"]
    split = Mesh(mesh.devices.reshape(docs, HK, contexts // HK), ("doc", "x", "z"))
    ctx = ("x", "z")
    rows = P(("doc",) + ctx, None)
    return jax.shard_map(
        on_device,
        mesh=split,
        in_specs=(rows, rows, rows, P("doc", ctx), P(ctx, None), P(ctx, None), P(ctx, None)),
        out_specs=(rows, P("doc", None)),
        check_vma=False,
    )
```

time: 111 us -> 94.8 us (0.85)
  Pallas kernels: 20.6 us -> 11.2 us
  blocking collectives: 53.2 us -> 47.3 us
  local copies, waits for them, and re-layouts: 1.25 us -> 0.01 us
    pallas_call x3, Pallas kernels: 16.1 us -> 9.32 us  [the longest x1 7.25 us: on_device(): pl.pallas_call(prefill_kernel, out_shape=(shape((block, HQ * HS), BF16),...]
    all_to_all x3, blocking collectives: 53.2 us -> 47.3 us  [the longest x1 22.5 us: on_device(): parts = in_vmem(lax.all_to_all(parts, 'z', 0, 0, tiled=True))]
    pallas_call x1, Pallas kernels: 2.14 us -> 0.43 us  [on_device(): call(combine_kernel, shape((nx, QROWS + 2 * block, HS), BF16), name='comb...]
    another operation x2 -> x0, local copies, waits for them, and re-layouts: 1.24 us -> none  [rotary_tables(): return (jnp.tile(cosine, (GROUP + 2, 1)), jnp.tile(sine, (GROUP + 2, 1)))]
where the time goes in v2:
time: 94.8 us; the launch traced here: 94 us
  blocking collectives  47.3 us (50%)
  waiting for transfers between devices  19.5 us (21%)
  starting transfers between devices  15.2 us (16%)
  Pallas kernels  11.2 us (12%)
    all_to_all x1, blocking collectives, on_device(): parts = in_vmem(lax.all_to_all(parts, 'z', 0, 0, tiled=True))  22.5 us
    all_to_all x1, waiting for transfers between devices, on_device(): sums = in_vmem(lax.all_to_all(spread, 'z', 0, 0, tiled=True))  19.5 us
    all_to_all x1, starting transfers between devices, on_device(): sums = in_vmem(lax.all_to_all(spread, 'z', 0, 0, tiled=True))  15.2 us
    all_to_all x1, blocking collectives, on_device(): cache = in_vmem(lax.all_to_all(slabs, 'x', 0, 0, tiled=True))  14.1 us
    all_to_all x1, blocking collectives, on_device(): heads = in_vmem(lax.all_to_all(heads, 'x', 0, 0, tiled=True))  10.7 us
    pallas_call x1, Pallas kernels, on_device(): pl.pallas_call(prefill_kernel, out_shape=(shape((block, HQ * HS), BF16),...  7.25 us
  transfers between devices with their start and end apart: 1, of which 1 were waited for; matrix products, arithmetic and copies ran while one was open for 0% of the time, Pallas kernels for 0%

profile of v2, /device:TPU:24, one launch (start us, length us, event | category | flops | bytes accessed | tf_op | source)
XLA Modules:
  0.0 94.0 jit_solution(8835745127373525807)
XLA Ops:
  0.6 1.5 %project.1 = bf16[4,560,128]{2,1,0:T(8,128)(2,1)S(1)} custom-call(bf16[4,64]{1,0:T(4,128)(2,1)} %embed_ref.1, bf16[64,2048]{1,0:T(8,128)(2,1)} %wq_ref.1, bf16[64,512]{1,0:T(8,128)(2,1)} %wk_ref.1, bf16[64,512]{1,0:T(8,128)(2,1)} %wv_ref.1, bf16[256,512]{1,0:T(8,128)(2,1)} %key_ref.3, bf16[256,512]{1,0:T(8,128)(2,1)} %value_ref.3), custom_call_target="tpu_custom_call" | custom-call | tf_op jit(solution)/shard_map/project/pallas_call | solution.py:249
  2.1 14.1 %all_to_all.20.in_ref.cache_ref = bf16[4,560,128]{2,1,0:T(8,128)(2,1)S(1)} all-to-all(bf16[4,560,128]{2,1,0:T(8,128)(2,1)S(1)} %project.1), channel_id=1, replica_groups=mesh['doc'=8,'x'=4,'z'=16] {'x'}, dimensions={0} | all-to-all | bytes 1146880 | tf_op jit(solution)/shard_map/all_to_all | solution.py:255
  16.2 0.7 spread.1
  16.9 15.2 %all-to-all-start.1 = ((bf16[16,80,128]{2,1,0:T(8,128)(2,1)}), bf16[16,80,128]{2,1,0:T(8,128)(2,1)S(1)}, u32[]{:S(2)}, u32[]{:S(2)}) async-start(bf16[16,80,128]{2,1,0:T(8,128)(2,1)} %spread.1), calls=%async_computation.1 | async-start | bytes 655360 | tf_op jit(solution)/shard_map/all_to_all | solution.py:262
  32.2 0.1 negate_select_fusion
  32.3 19.5 %all-to-all-done.1.sums_ref = bf16[16,80,128]{2,1,0:T(8,128)(2,1)S(1)} async-done(((bf16[16,80,128]{2,1,0:T(8,128)(2,1)}), bf16[16,80,128]{2,1,0:T(8,128)(2,1)S(1)}, u32[]{:S(2)}, u32[]{:S(2)}) %all-to-all-start.1) | async-done | bytes 327712 | tf_op jit(solution)/shard_map/all_to_all | solution.py:262
  51.8 1.3 %decode.1 = (bf16[16,56,128]{2,1,0:T(8,128)(2,1)S(1)}, f32[3,16,128]{2,1,0:T(8,128)S(1)}) custom-call(bf16[16,80,128]{2,1,0:T(8,128)(2,1)S(1)} %all-to-all-done.1.sums_ref, bf16[4,560,128]{2,1,0:T(8,128)(2,1)S(1)} %all_to_all.20.in_ref.cache_ref, f32[24,128]{1,0:T(8,128)S(1)} %get-tuple-element.7.cos_ref, f32[24,128]{1,0:T(8,128)S(1)} %get-tuple-element.6.sin_ref), custom_call_target="tpu_custom_call" | custom-call | tf_op jit(solution)/shard_map/decode/pallas_call | solution.py:263
  53.1 22.5 %all_to_all.21.parts_ref = bf16[16,56,128]{2,1,0:T(8,128)(2,1)S(1)} all-to-all(bf16[16,56,128]{2,1,0:T(8,128)(2,1)S(1)} %get-tuple-element.4), channel_id=1, replica_groups=mesh['doc'=8,'x'=4,'z'=16] {'z'}, dimensions={0} | all-to-all | bytes 458752 | tf_op jit(solution)/shard_map/all_to_all | solution.py:269
  75.7 0.0 copy-start
  75.7 0.4 combine.1
  76.1 0.0 copy-start.1
  76.1 0.0 copy-start.2
  76.1 10.7 %all_to_all.22.anchor_ref = bf16[4,528,128]{2,1,0:T(8,128)(2,1)S(1)} all-to-all(bf16[4,528,128]{2,1,0:T(8,128)(2,1)S(1)} %combine.1), channel_id=1, replica_groups=mesh['doc'=8,'x'=4,'z'=16] {'x'}, dimensions={0} | all-to-all | bytes 1081344 | tf_op jit(solution)/shard_map/all_to_all | solution.py:276
  86.8 0.0 copy-done
  86.8 0.0 copy-done.1
  86.8 0.0 copy-done.2
  86.8 7.3 %prefill.1 = (bf16[256,2048]{1,0:T(8,128)(2,1)}, bf16[4,2048]{1,0:T(4,128)(2,1)}) custom-call(bf16[256,2048]{1,0:T(8,128)(2,1)S(1)} %copy-done, bf16[256,512]{1,0:T(8,128)(2,1)S(1)} %copy-done.1, bf16[256,512]{1,0:T(8,128)(2,1)S(1)} %copy-done.2, bf16[4,528,128]{2,1,0:T(8,128)(2,1)S(1)} %all_to_all.22.anchor_ref), custom_call_target="tpu_custom_call" | custom-call | tf_op jit(solution)/shard_map/prefill/pallas_call | solution.py:278
  (4 shorter events, 0.0 us)
Async XLA Ops:
  16.9 34.8 %all-to-all-start.1 = ((bf16[16,80,128]{2,1,0:T(8,128)(2,1)}), bf16[16,80,128]{2,1,0:T(8,128)(2,1)S(1)}, u32[]{:S(2)}, u32[]{:S(2)}) async-start(bf16[16,80,128]{2,1,0:T(8,128)(2,1)} %spread.1), calls=%async_computation.1 | async-start | bytes 655360 | tf_op jit(solution)/shard_map/all_to_all | solution.py:262
  75.7 11.1 %copy-start = (bf16[256,2048]{1,0:T(8,128)(2,1)S(1)}, bf16[256,2048]{1,0:T(8,128)(2,1)}, u32[]{:S(2)}) copy-start(bf16[256,2048]{1,0:T(8,128)(2,1)} %query_ref.1) | copy-start | bytes 3145732
  76.1 10.7 %copy-start.1 = (bf16[256,512]{1,0:T(8,128)(2,1)S(1)}, bf16[256,512]{1,0:T(8,128)(2,1)}, u32[]{:S(2)}) copy-start(bf16[256,512]{1,0:T(8,128)(2,1)} %key_ref.3) | copy-start | bytes 786436
  76.1 10.7 %copy-start.2 = (bf16[256,512]{1,0:T(8,128)(2,1)S(1)}, bf16[256,512]{1,0:T(8,128)(2,1)}, u32[]{:S(2)}) copy-start(bf16[256,512]{1,0:T(8,128)(2,1)} %value_ref.3) | copy-start | bytes 786436

commit v3 on v2

--- a/solution.py
+++ b/solution.py
@@ -17,6 +17,7 @@
 QROWS = GROUP * STEPS
 PROWS = QROWS + 2 * STEPS
 SROWS = QROWS // 2
+HROWS = 2 * QROWS + SROWS
 SCALE = 1.0 / math.sqrt(HS)
 EXP2_SCALE = SCALE * math.log2(math.e)
 BF16 = jnp.bfloat16
@@ -45,7 +46,8 @@
 
 
 def project_kernel(embed_ref, wq_ref, wk_ref, wv_ref, key_ref, value_ref, out_ref, part_ref):
-    block = key_ref.shape[0]
+    parities = out_ref.shape[0] // HK
+    half = key_ref.shape[0] // parities
     embed = embed_ref[...]
     query, key, value = dot(embed, wq_ref[...]), dot(embed, wk_ref[...]), dot(embed, wv_ref[...])
     for group in range(HK):
@@ -55,24 +57,31 @@
             part_ref[group, j * STEPS : (j + 1) * STEPS] = query[:, head * HS : (head + 1) * HS]
         part_ref[group, QROWS : QROWS + STEPS] = key[:, cols]
         part_ref[group, QROWS + STEPS : PROWS] = value[:, cols]
-        out_ref[group, 2 * PROWS : 2 * PROWS + block] = key_ref[:, cols]
-        out_ref[group, 2 * PROWS + block : 2 * PROWS + 2 * block] = value_ref[:, cols]
+        for parity in range(parities):
+            near = group * parities + parity
+            rows = slice(parity * half, (parity + 1) * half)
+            out_ref[near, 2 * PROWS : 2 * PROWS + half] = key_ref[rows, cols]
+            out_ref[near, 2 * PROWS + half : 2 * PROWS + 2 * half] = value_ref[rows, cols]
     for group in range(HK):
         high, low = split2(part_ref[group])
-        out_ref[group, 0:PROWS] = high
-        out_ref[group, PROWS : 2 * PROWS] = low
-
-
-def spread_kernel(in_ref, out_ref):
-    sources = in_ref.shape[0]
-    peers = out_ref.shape[0]
-    piece = (in_ref.shape[1] - 2 * PROWS) // peers
+        for parity in range(parities):
+            out_ref[group * parities + parity, 0:PROWS] = high
+            out_ref[group * parities + parity, PROWS : 2 * PROWS] = low
+
+
+def add_projections(in_ref):
     total = in_ref[0, 0:PROWS].astype(F32) + in_ref[0, PROWS : 2 * PROWS].astype(F32)
-    for source in range(1, sources):
+    for source in range(1, in_ref.shape[0]):
         total = total + (
             in_ref[source, 0:PROWS].astype(F32) + in_ref[source, PROWS : 2 * PROWS].astype(F32)
         )
-    high, low = split2(total)
+    return total
+
+
+def spread_kernel(in_ref, out_ref):
+    peers = out_ref.shape[0]
+    piece = out_ref.shape[1] - 2 * PROWS
+    high, low = split2(add_projections(in_ref))
     for peer in range(peers):
         out_ref[peer, 0:PROWS] = high
         out_ref[peer, PROWS : 2 * PROWS] = low
@@ -80,39 +89,52 @@
         out_ref[peer, 2 * PROWS : 2 * PROWS + piece] = in_ref[0, start : start + piece]
 
 
-def decode_kernel(sums_ref, cache_ref, cos_ref, sin_ref, out_ref, new_ref):
-    peers = sums_ref.shape[0]
-    blocks = cache_ref.shape[0]
-    block = (cache_ref.shape[1] - 2 * PROWS) // 2
-    piece = sums_ref.shape[1] - 2 * PROWS
-    total = sums_ref[0, 0:PROWS].astype(F32) + sums_ref[0, PROWS : 2 * PROWS].astype(F32)
-    for peer in range(1, peers):
-        total = total + (
-            sums_ref[peer, 0:PROWS].astype(F32) + sums_ref[peer, PROWS : 2 * PROWS].astype(F32)
-        )
-    rotated = total * cos_ref[...] + pltpu.roll(total, HS // 2, 1) * sin_ref[...]
-    query = rotated[0:QROWS].astype(BF16)
-    parts = []
-    for c in range(blocks):
-        keys = cache_ref[c, 2 * PROWS : 2 * PROWS + block]
-        values = cache_ref[c, 2 * PROWS + block : 2 * PROWS + 2 * block]
-        scores = dot_t(query, keys) * SCALE
-        part_max = jnp.max(scores, axis=1, keepdims=True)
-        weights = jnp.exp(scores - part_max)
-        part_sum = jnp.sum(weights, axis=1, keepdims=True)
-        parts.append((part_max, part_sum, dot(weights.astype(BF16), values)))
+def pack_stats(part_max, part_sum):
+    lane = lax.broadcasted_iota(jnp.int32, (QROWS, HS), 1)
+    stats = jnp.zeros((QROWS, HS), F32)
+    for at, value in enumerate(split3(part_max) + split3(part_sum)):
+        stats = jnp.where(lane == at, value.astype(F32), stats)
+    stats = jnp.where(lane[:SROWS] < HS // 2, stats[:SROWS], pltpu.roll(stats[SROWS:], HS // 2, 1))
+    return stats.astype(BF16)
+
+
+def unpack_stats(stats):
+    stats = stats.astype(F32)
+    stats = jnp.concatenate([stats, pltpu.roll(stats, HS // 2, 1)], axis=0)
+    return (
+        stats[:, 0:1] + stats[:, 1:2] + stats[:, 2:3],
+        stats[:, 3:4] + stats[:, 4:5] + stats[:, 5:6],
+    )
+
+
+def join(parts):
     joint_max = functools.reduce(jnp.maximum, [part[0] for part in parts])
     joint_sum, joint_out = 0.0, 0.0
     for part_max, part_sum, part_out in parts:
         factor = jnp.exp(part_max - joint_max)
         joint_sum = joint_sum + part_sum * factor
         joint_out = joint_out + part_out * factor
-    lane = lax.broadcasted_iota(jnp.int32, (QROWS, HS), 1)
-    stats = jnp.zeros((QROWS, HS), F32)
-    for at, value in enumerate(split3(joint_max) + split3(joint_sum)):
-        stats = jnp.where(lane == at, value.astype(F32), stats)
-    stats = jnp.where(lane[:SROWS] < HS // 2, stats[:SROWS], pltpu.roll(stats[SROWS:], HS // 2, 1))
-    stats = stats.astype(BF16)
+    return joint_max, joint_sum, joint_out
+
+
+def decode_kernel(sums_ref, cache_ref, cos_ref, sin_ref, out_ref, new_ref):
+    peers = sums_ref.shape[0]
+    half = (cache_ref.shape[1] - 2 * PROWS) // 2
+    piece = sums_ref.shape[1] - 2 * PROWS
+    total = add_projections(sums_ref)
+    rotated = total * cos_ref[...] + pltpu.roll(total, HS // 2, 1) * sin_ref[...]
+    query = rotated[0:QROWS].astype(BF16)
+    parts = []
+    for c in range(cache_ref.shape[0]):
+        keys = cache_ref[c, 2 * PROWS : 2 * PROWS + half]
+        values = cache_ref[c, 2 * PROWS + half : 2 * PROWS + 2 * half]
+        scores = dot_t(query, keys) * SCALE
+        part_max = jnp.max(scores, axis=1, keepdims=True)
+        weights = jnp.exp(scores - part_max)
+        part_sum = jnp.sum(weights, axis=1, keepdims=True)
+        parts.append((part_max, part_sum, dot(weights.astype(BF16), values)))
+    joint_max, joint_sum, joint_out = join(parts)
+    stats = pack_stats(joint_max, joint_sum)
     joint_out = joint_out.astype(BF16)
     anchor = sums_ref[0, 2 * PROWS : 2 * PROWS + piece]
     for peer in range(peers):
@@ -137,38 +159,50 @@
     peers = parts_ref.shape[0]
     first = QROWS + SROWS
     piece = parts_ref.shape[1] - first
-    maxima, sums = [], []
+    parts = []
     for peer in range(peers):
-        stats = parts_ref[peer, QROWS:first].astype(F32)
-        stats = jnp.concatenate([stats, pltpu.roll(stats, HS // 2, 1)], axis=0)
-        maxima.append(stats[:, 0:1] + stats[:, 1:2] + stats[:, 2:3])
-        sums.append(stats[:, 3:4] + stats[:, 4:5] + stats[:, 5:6])
+        part_max, part_sum = unpack_stats(parts_ref[peer, QROWS:first])
+        parts.append((part_max, part_sum, parts_ref[peer, 0:QROWS].astype(F32)))
+    has_new = lax.axis_index("zo") == 0
     new_max = new_ref[0][:, 0:1]
-    global_max = functools.reduce(jnp.maximum, maxima + [new_max])
-    factor = jnp.exp(new_max - global_max)
-    total_sum = new_ref[1][:, 0:1] * factor
-    total_out = new_ref[2] * factor
-    for peer in range(peers):
-        factor = jnp.exp(maxima[peer] - global_max)
-        total_sum = total_sum + sums[peer] * factor
-        total_out = total_out + parts_ref[peer, 0:QROWS].astype(F32) * factor
-    decoded = (total_out / total_sum).astype(BF16)
-    for x in range(out_ref.shape[0]):
-        out_ref[x, 0:QROWS] = decoded
+    parts.append(
+        (
+            jnp.where(has_new, new_max, parts[0][0]),
+            jnp.where(has_new, new_ref[1][:, 0:1], 0.0),
+            jnp.where(has_new, new_ref[2], 0.0),
+        )
+    )
+    joint_max, joint_sum, joint_out = join(parts)
+    high, low = split2(joint_out)
+    stats = pack_stats(joint_max, joint_sum)
+    for near in range(out_ref.shape[0]):
+        out_ref[near, 0:QROWS] = high
+        out_ref[near, QROWS : 2 * QROWS] = low
+        out_ref[near, 2 * QROWS : HROWS] = stats
         for peer in range(peers):
-            start = QROWS + peer * piece
-            out_ref[x, start : start + piece] = parts_ref[peer, first : first + piece]
+            start = HROWS + peer * piece
+            out_ref[near, start : start + piece] = parts_ref[peer, first : first + piece]
 
 
 def prefill_kernel(query_ref, key_ref, value_ref, anchor_ref, out_ref, decoded_ref):
     block = key_ref.shape[0]
     half = block // 2
     group = pl.program_id(0)
-    use_anchor = (lax.axis_index("x") + lax.axis_index("z")) != 0
+    parities = anchor_ref.shape[0] // HK
+    piece = (anchor_ref.shape[1] - HROWS) // 2
+    use_anchor = (lax.axis_index("x") + lax.axis_index("zz") + lax.axis_index("zo")) != 0
     head_cols = pl.ds(pl.multiple_of(group * HS, HS), HS)
     key = key_ref[:, head_cols]
-    anchor_key = anchor_ref[group, QROWS : QROWS + block]
-    anchor_value = anchor_ref[group, QROWS + block : QROWS + 2 * block]
+    near = [group * parities + parity for parity in range(parities)]
+    anchor_key = jnp.concatenate([anchor_ref[n, HROWS : HROWS + piece] for n in near], axis=0)
+    anchor_value = jnp.concatenate([anchor_ref[n, HROWS + piece :] for n in near], axis=0)
+    parts = []
+    for n in near:
+        part_max, part_sum = unpack_stats(anchor_ref[n, 2 * QROWS : HROWS])
+        part_out = anchor_ref[n, 0:QROWS].astype(F32) + anchor_ref[n, QROWS : 2 * QROWS].astype(F32)
+        parts.append((part_max, part_sum, part_out))
+    _, decoded_sum, decoded_out = join(parts)
+    decoded = (decoded_out / decoded_sum).astype(BF16)
     values = jnp.concatenate([anchor_value.T, value_ref[:, head_cols].T], axis=1)
     causal = lax.broadcasted_iota(jnp.int32, (half, half), 0) <= lax.broadcasted_iota(
         jnp.int32, (half, half), 1
@@ -206,7 +240,7 @@
             lax.broadcasted_iota(jnp.int32, (STEPS, QROWS), 1)
             == lax.broadcasted_iota(jnp.int32, (STEPS, QROWS), 0) + j * STEPS
         )
-        decoded_ref[:, cols] = dot(pick.astype(BF16), anchor_ref[group, 0:QROWS]).astype(BF16)
+        decoded_ref[:, cols] = dot(pick.astype(BF16), decoded).astype(BF16)
 
 
 def rotary_tables(position):
@@ -241,39 +275,41 @@
 
 def on_device(ctx_query, ctx_key, ctx_value, step_embed, w_query, w_key, w_value):
     block = ctx_query.shape[0]
-    nx, nz = lax.axis_size("x"), lax.axis_size("z")
-    piece = 2 * block // nz
+    parities, far = lax.axis_size("zo"), lax.axis_size("zz")
+    near = lax.axis_size("x") * parities
+    half = block // parities
+    piece = 2 * half // far
     shape = jax.ShapeDtypeStruct
-    cosine, sine = rotary_tables(nx * nz * block)
+    cosine, sine = rotary_tables(near * far * block)
 
     slabs = call(
         project_kernel,
-        shape((nx, 2 * PROWS + 2 * block, HS), BF16),
+        shape((near, 2 * PROWS + 2 * half, HS), BF16),
         name="project",
         scratch_shapes=[pltpu.VMEM((HK, PROWS, HS), F32)],
     )(step_embed, w_query, w_key, w_value, ctx_key, ctx_value)
-    cache = in_vmem(lax.all_to_all(slabs, "x", 0, 0, tiled=True))
+    cache = in_vmem(lax.all_to_all(slabs, ("x", "zo"), 0, 0, tiled=True))
     spread = call(
         spread_kernel,
-        shape((nz, 2 * PROWS + piece, HS), BF16),
+        shape((far, 2 * PROWS + piece, HS), BF16),
         name="spread",
         in_specs=[VMEM_SPEC],
     )(cache)
-    sums = in_vmem(lax.all_to_all(spread, "z", 0, 0, tiled=True))
+    sums = in_vmem(lax.all_to_all(spread, "zz", 0, 0, tiled=True))
     parts, new = call(
         decode_kernel,
-        (shape((nz, QROWS + SROWS + piece, HS), BF16), shape((3, QROWS, HS), F32)),
+        (shape((far, QROWS + SROWS + piece, HS), BF16), shape((3, QROWS, HS), F32)),
         name="decode",
         in_specs=[VMEM_SPEC] * 4,
     )(sums, cache, in_vmem(cosine), in_vmem(sine))
-    parts = in_vmem(lax.all_to_all(parts, "z", 0, 0, tiled=True))
+    parts = in_vmem(lax.all_to_all(parts, "zz", 0, 0, tiled=True))
     heads = call(
         combine_kernel,
-        shape((nx, QROWS + 2 * block, HS), BF16),
+        shape((near, HROWS + 2 * half, HS), BF16),
         name="combine",
         in_specs=[VMEM_SPEC] * 2,
     )(parts, in_vmem(new))
-    heads = in_vmem(lax.all_to_all(heads, "x", 0, 0, tiled=True))
+    heads = in_vmem(lax.all_to_all(heads, ("x", "zo"), 0, 0, tiled=True))
     width = GROUP * HS
     context_out, decoded = pl.pallas_call(
         prefill_kernel,
@@ -292,8 +328,8 @@
 
 def solution(mesh):
     docs, contexts = mesh.shape["doc"], mesh.shape["ctx"]
-    split = Mesh(mesh.devices.reshape(docs, HK, contexts // HK), ("doc", "x", "z"))
-    ctx = ("x", "z")
+    split = Mesh(mesh.devices.reshape(docs, HK, contexts // (2 * HK), 2), ("doc", "x", "zz", "zo"))
+    ctx = ("x", "zz", "zo")
     rows = P(("doc",) + ctx, None)
     return jax.shard_map(
         on_device,

time: 94.8 us -> 88.3 us (0.931)
  waiting for transfers between devices: 19.5 us -> 14.6 us
  starting transfers between devices: 15.2 us -> 14.2 us
    all_to_all x1, waiting for transfers between devices: 19.5 us -> 14.6 us  [on_device(): sums = in_vmem(lax.all_to_all(spread, 'zz', 0, 0, tiled=True))]
    all_to_all x1, starting transfers between devices: 15.2 us -> 14.2 us  [on_device(): sums = in_vmem(lax.all_to_all(spread, 'zz', 0, 0, tiled=True))]
where the time goes in v3:
time: 88.3 us; the launch traced here: 88 us
  blocking collectives  46.4 us (53%)
  waiting for transfers between devices  14.6 us (17%)
  starting transfers between devices  14.2 us (16%)
  Pallas kernels  12 us (14%)
    all_to_all x1, blocking collectives, on_device(): parts = in_vmem(lax.all_to_all(parts, 'zz', 0, 0, tiled=True))  17.3 us
    all_to_all x1, blocking collectives, on_device(): cache = in_vmem(lax.all_to_all(slabs, ('x', 'zo'), 0, 0, tiled=True))  16.7 us
    all_to_all x1, waiting for transfers between devices, on_device(): sums = in_vmem(lax.all_to_all(spread, 'zz', 0, 0, tiled=True))  14.6 us
    all_to_all x1, starting transfers between devices, on_device(): sums = in_vmem(lax.all_to_all(spread, 'zz', 0, 0, tiled=True))  14.2 us
    all_to_all x1, blocking collectives, on_device(): heads = in_vmem(lax.all_to_all(heads, ('x', 'zo'), 0, 0, tiled=True))  12.3 us
    pallas_call x1, Pallas kernels, on_device(): pl.pallas_call(prefill_kernel, out_shape=(shape((block, HQ * HS), BF16),...  7.19 us
    pallas_call x1, Pallas kernels, on_device(): call(decode_kernel, (shape((far, QROWS + SROWS + piece, HS), BF16), shape...  2.23 us
  transfers between devices with their start and end apart: 1, of which 1 were waited for; matrix products, arithmetic and copies ran while one was open for 0% of the time, Pallas kernels for 0%

profile of v3, /device:TPU:24, one launch (start us, length us, event | category | flops | bytes accessed | tf_op | source)
XLA Modules:
  0.0 88.0 jit_solution(13010393537749034425)
XLA Ops:
  0.6 1.5 %project.1 = bf16[8,304,128]{2,1,0:T(8,128)(2,1)S(1)} custom-call(bf16[4,64]{1,0:T(4,128)(2,1)} %embed_ref.1, bf16[64,2048]{1,0:T(8,128)(2,1)} %wq_ref.1, bf16[64,512]{1,0:T(8,128)(2,1)} %wk_ref.1, bf16[64,512]{1,0:T(8,128)(2,1)} %wv_ref.1, bf16[256,512]{1,0:T(8,128)(2,1)} %key_ref.3, bf16[256,512]{1,0:T(8,128)(2,1)} %value_ref.3), custom_call_target="tpu_custom_call" | custom-call | tf_op jit(solution)/shard_map/project/pallas_call | solution.py:285
  2.1 16.7 %all_to_all.20.in_ref.cache_ref = bf16[8,304,128]{2,1,0:T(8,128)(2,1)S(1)} all-to-all(bf16[8,304,128]{2,1,0:T(8,128)(2,1)S(1)} %project.1), channel_id=1, replica_groups=mesh['doc'=8,'x'=4,'zz'=8,'zo'=2] {'x','zo'}, dimensions={0} | all-to-all | bytes 1245184 | tf_op jit(solution)/shard_map/all_to_all | solution.py:291
  18.8 0.7 spread.1
  19.5 14.2 %all-to-all-start.1 = ((bf16[8,80,128]{2,1,0:T(8,128)(2,1)}), bf16[8,80,128]{2,1,0:T(8,128)(2,1)S(1)}, u32[]{:S(2)}, u32[]{:S(2)}) async-start(bf16[8,80,128]{2,1,0:T(8,128)(2,1)} %spread.1), calls=%async_computation.1 | async-start | bytes 327680 | tf_op jit(solution)/shard_map/all_to_all | solution.py:298
  33.8 0.1 negate_select_fusion
  33.9 14.6 %all-to-all-done.1.sums_ref = bf16[8,80,128]{2,1,0:T(8,128)(2,1)S(1)} async-done(((bf16[8,80,128]{2,1,0:T(8,128)(2,1)}), bf16[8,80,128]{2,1,0:T(8,128)(2,1)S(1)}, u32[]{:S(2)}, u32[]{:S(2)}) %all-to-all-start.1) | async-done | bytes 163872 | tf_op jit(solution)/shard_map/all_to_all | solution.py:298
  48.5 2.2 %decode.1 = (bf16[8,56,128]{2,1,0:T(8,128)(2,1)S(1)}, f32[3,16,128]{2,1,0:T(8,128)S(1)}) custom-call(bf16[8,80,128]{2,1,0:T(8,128)(2,1)S(1)} %all-to-all-done.1.sums_ref, bf16[8,304,128]{2,1,0:T(8,128)(2,1)S(1)} %all_to_all.20.in_ref.cache_ref, f32[24,128]{1,0:T(8,128)S(1)} %get-tuple-element.7.cos_ref, f32[24,128]{1,0:T(8,128)S(1)} %get-tuple-element.6.sin_ref), custom_call_target="tpu_custom_call" | custom-call | tf_op jit(solution)/shard_map/decode/pallas_call | solution.py:299
  50.7 0.0 copy-start
  50.7 17.3 %all_to_all.21.parts_ref = bf16[8,56,128]{2,1,0:T(8,128)(2,1)S(1)} all-to-all(bf16[8,56,128]{2,1,0:T(8,128)(2,1)S(1)} %get-tuple-element.4), channel_id=1, replica_groups=mesh['doc'=8,'x'=4,'zz'=8,'zo'=2] {'zz'}, dimensions={0} | all-to-all | bytes 229376 | tf_op jit(solution)/shard_map/all_to_all | solution.py:305
  68.1 0.4 combine.1
  68.5 0.0 copy-start.1
  68.5 0.0 copy-start.2
  68.5 12.3 %all_to_all.22.anchor_ref = bf16[8,296,128]{2,1,0:T(8,128)(2,1)S(1)} all-to-all(bf16[8,296,128]{2,1,0:T(8,128)(2,1)S(1)} %combine.1), channel_id=1, replica_groups=mesh['doc'=8,'x'=4,'zz'=8,'zo'=2] {'x','zo'}, dimensions={0} | all-to-all | bytes 1212416 | tf_op jit(solution)/shard_map/all_to_all | solution.py:312
  80.8 0.0 copy-done
  80.8 0.0 copy-done.1
  80.8 0.0 copy-done.2
  80.8 7.2 %prefill.1 = (bf16[256,2048]{1,0:T(8,128)(2,1)}, bf16[4,2048]{1,0:T(4,128)(2,1)}) custom-call(bf16[256,2048]{1,0:T(8,128)(2,1)S(1)} %copy-done, bf16[256,512]{1,0:T(8,128)(2,1)S(1)} %copy-done.1, bf16[256,512]{1,0:T(8,128)(2,1)S(1)} %copy-done.2, bf16[8,296,128]{2,1,0:T(8,128)(2,1)S(1)} %all_to_all.22.anchor_ref), custom_call_target="tpu_custom_call" | custom-call | tf_op jit(solution)/shard_map/prefill/pallas_call | solution.py:314
  (4 shorter events, 0.0 us)
Async XLA Ops:
  19.5 29.0 %all-to-all-start.1 = ((bf16[8,80,128]{2,1,0:T(8,128)(2,1)}), bf16[8,80,128]{2,1,0:T(8,128)(2,1)S(1)}, u32[]{:S(2)}, u32[]{:S(2)}) async-start(bf16[8,80,128]{2,1,0:T(8,128)(2,1)} %spread.1), calls=%async_computation.1 | async-start | bytes 327680 | tf_op jit(solution)/shard_map/all_to_all | solution.py:298
  50.7 30.0 %copy-start = (bf16[256,2048]{1,0:T(8,128)(2,1)S(1)}, bf16[256,2048]{1,0:T(8,128)(2,1)}, u32[]{:S(2)}) copy-start(bf16[256,2048]{1,0:T(8,128)(2,1)} %query_ref.1) | copy-start | bytes 3145732
  68.5 12.3 %copy-start.1 = (bf16[256,512]{1,0:T(8,128)(2,1)S(1)}, bf16[256,512]{1,0:T(8,128)(2,1)}, u32[]{:S(2)}) copy-start(bf16[256,512]{1,0:T(8,128)(2,1)} %key_ref.3) | copy-start | bytes 786436
  68.5 12.3 %copy-start.2 = (bf16[256,512]{1,0:T(8,128)(2,1)S(1)}, bf16[256,512]{1,0:T(8,128)(2,1)}, u32[]{:S(2)}) copy-start(bf16[256,512]{1,0:T(8,128)(2,1)} %value_ref.3) | copy-start | bytes 786436

commit v4 on v3

--- a/solution.py
+++ b/solution.py
@@ -124,16 +124,22 @@
     total = add_projections(sums_ref)
     rotated = total * cos_ref[...] + pltpu.roll(total, HS // 2, 1) * sin_ref[...]
     query = rotated[0:QROWS].astype(BF16)
-    parts = []
-    for c in range(cache_ref.shape[0]):
-        keys = cache_ref[c, 2 * PROWS : 2 * PROWS + half]
-        values = cache_ref[c, 2 * PROWS + half : 2 * PROWS + 2 * half]
-        scores = dot_t(query, keys) * SCALE
-        part_max = jnp.max(scores, axis=1, keepdims=True)
-        weights = jnp.exp(scores - part_max)
-        part_sum = jnp.sum(weights, axis=1, keepdims=True)
-        parts.append((part_max, part_sum, dot(weights.astype(BF16), values)))
-    joint_max, joint_sum, joint_out = join(parts)
+    sources = range(cache_ref.shape[0])
+    scores = jnp.concatenate(
+        [dot_t(query, cache_ref[c, 2 * PROWS : 2 * PROWS + half]) for c in sources], axis=1
+    )
+    scores = scores * SCALE
+    joint_max = jnp.max(scores, axis=1, keepdims=True)
+    weights = jnp.exp(scores - joint_max)
+    joint_sum = jnp.sum(weights, axis=1, keepdims=True)
+    weights = weights.astype(BF16)
+    joint_out = functools.reduce(
+        jnp.add,
+        [
+            dot(weights[:, c * half : (c + 1) * half], cache_ref[c, 2 * PROWS + half :])
+            for c in sources
+        ],
+    )
     stats = pack_stats(joint_max, joint_sum)
     joint_out = joint_out.astype(BF16)
     anchor = sums_ref[0, 2 * PROWS : 2 * PROWS + piece]
@@ -184,18 +190,69 @@
             out_ref[near, start : start + piece] = parts_ref[peer, first : first + piece]
 
 
-def prefill_kernel(query_ref, key_ref, value_ref, anchor_ref, out_ref, decoded_ref):
-    block = key_ref.shape[0]
-    half = block // 2
+def own_kernel(query_ref, key_ref, value_ref, out_ref, stats_ref):
+    half = key_ref.shape[0] // 2
+    key = key_ref[...]
+    values = value_ref[...].T
+    causal = lax.broadcasted_iota(jnp.int32, (half, half), 0) <= lax.broadcasted_iota(
+        jnp.int32, (half, half), 1
+    )
+    for j in range(GROUP):
+        query = query_ref[:, j * HS : (j + 1) * HS]
+        early = dot_t(key[:half], query)
+        late = dot_t(key[half:], query[half:])
+        for part in range(2):
+            rows = slice(part * half, (part + 1) * half)
+            if part == 0:
+                scores = jnp.where(causal, early[:, rows], -jnp.inf)
+            else:
+                late = jnp.where(causal, late, -jnp.inf)
+                scores = jnp.concatenate([early[:, rows], late], axis=0)
+            own_max = jnp.max(scores, axis=0, keepdims=True)
+            weights = jnp.exp2((scores - own_max) * EXP2_SCALE)
+            stats_ref[j, 0:1, rows] = own_max
+            stats_ref[j, 1:2, rows] = jnp.sum(weights, axis=0, keepdims=True)
+            out_ref[j, :, rows] = dot(values[:, : (part + 1) * half], weights.astype(BF16))
+
+
+def prefill_kernel(query_ref, own_ref, own_stats_ref, anchor_ref, out_ref, decoded_ref):
     group = pl.program_id(0)
     parities = anchor_ref.shape[0] // HK
     piece = (anchor_ref.shape[1] - HROWS) // 2
     use_anchor = (lax.axis_index("x") + lax.axis_index("zz") + lax.axis_index("zo")) != 0
-    head_cols = pl.ds(pl.multiple_of(group * HS, HS), HS)
-    key = key_ref[:, head_cols]
     near = [group * parities + parity for parity in range(parities)]
-    anchor_key = jnp.concatenate([anchor_ref[n, HROWS : HROWS + piece] for n in near], axis=0)
-    anchor_value = jnp.concatenate([anchor_ref[n, HROWS + piece :] for n in near], axis=0)
+    keys = jnp.concatenate([anchor_ref[n, HROWS : HROWS + piece] for n in near], axis=0)
+    values = jnp.concatenate([anchor_ref[n, HROWS + piece :] for n in near], axis=0).T
+
+    half = out_ref.shape[0] // 2
+    units = [(j, slice(part * half, (part + 1) * half)) for j in range(GROUP) for part in range(2)]
+
+    def scores_of(j, rows):
+        return dot_t(keys, query_ref[rows, j * HS : (j + 1) * HS])
+
+    def weigh(scores, j, rows):
+        own_max, own_sum = own_stats_ref[j, 0:1, rows], own_stats_ref[j, 1:2, rows]
+        anchor_max = jnp.max(scores, axis=0, keepdims=True)
+        row_max = jnp.where(use_anchor, jnp.maximum(own_max, anchor_max), own_max)
+        shift = jnp.where(use_anchor, row_max, jnp.inf)
+        weights = jnp.exp2((scores - shift) * EXP2_SCALE)
+        own_factor = jnp.exp2((own_max - row_max) * EXP2_SCALE)
+        row_sum = own_sum * own_factor + jnp.sum(weights, axis=0, keepdims=True)
+        return weights.astype(BF16), own_factor, 1.0 / row_sum
+
+    def finish(weighed, j, rows):
+        weights, own_factor, inverse = weighed
+        weighted = own_ref[j, :, rows] * own_factor + dot(values, weights)
+        out_ref[rows, j * HS : (j + 1) * HS] = (weighted * inverse).T.astype(BF16)
+
+    scores, weighed = scores_of(*units[0]), None
+    for at, unit in enumerate(units):
+        later = scores_of(*units[at + 1]) if at + 1 < len(units) else None
+        weighing = weigh(scores, *unit)
+        if weighed is not None:
+            finish(weighed, *units[at - 1])
+        scores, weighed = later, weighing
+    finish(weighed, *units[-1])
     parts = []
     for n in near:
         part_max, part_sum = unpack_stats(anchor_ref[n, 2 * QROWS : HROWS])
@@ -203,44 +260,12 @@
         parts.append((part_max, part_sum, part_out))
     _, decoded_sum, decoded_out = join(parts)
     decoded = (decoded_out / decoded_sum).astype(BF16)
-    values = jnp.concatenate([anchor_value.T, value_ref[:, head_cols].T], axis=1)
-    causal = lax.broadcasted_iota(jnp.int32, (half, half), 0) <= lax.broadcasted_iota(
-        jnp.int32, (half, half), 1
-    )
     for j in range(GROUP):
-        cols = slice(j * HS, (j + 1) * HS)
-        query = query_ref[:, pl.ds(pl.multiple_of((group * GROUP + j) * HS, HS), HS)]
-        anchor_scores = dot_t(anchor_key, query)
-        early_scores = dot_t(key[:half], query)
-        late_scores = dot_t(key[half:], query[half:])
-        for part in range(2):
-            rows = slice(part * half, (part + 1) * half)
-            anchor = anchor_scores[:, rows]
-            if part == 0:
-                own = jnp.where(causal, early_scores[:, rows], -jnp.inf)
-            else:
-                own = jnp.concatenate(
-                    [early_scores[:, rows], jnp.where(causal, late_scores, -jnp.inf)], axis=0
-                )
-            own_max = jnp.max(own, axis=0, keepdims=True)
-            anchor_max = jnp.max(anchor, axis=0, keepdims=True)
-            row_max = jnp.where(use_anchor, jnp.maximum(own_max, anchor_max), own_max)
-            anchor_shift = jnp.where(use_anchor, row_max, jnp.inf)
-            own_weights = jnp.exp2((own - row_max) * EXP2_SCALE)
-            anchor_weights = jnp.exp2((anchor - anchor_shift) * EXP2_SCALE)
-            row_sum = jnp.sum(own_weights, axis=0, keepdims=True) + jnp.sum(
-                anchor_weights, axis=0, keepdims=True
-            )
-            weights = jnp.concatenate(
-                [anchor_weights.astype(BF16), own_weights.astype(BF16)], axis=0
-            )
-            weighted = dot(values[:, : block + (part + 1) * half], weights)
-            out_ref[rows, cols] = (weighted * (1.0 / row_sum)).T.astype(BF16)
         pick = (
             lax.broadcasted_iota(jnp.int32, (STEPS, QROWS), 1)
             == lax.broadcasted_iota(jnp.int32, (STEPS, QROWS), 0) + j * STEPS
         )
-        decoded_ref[:, cols] = dot(pick.astype(BF16), decoded).astype(BF16)
+        decoded_ref[:, j * HS : (j + 1) * HS] = dot(pick.astype(BF16), decoded).astype(BF16)
 
 
 def rotary_tables(position):
@@ -296,6 +321,21 @@
         in_specs=[VMEM_SPEC],
     )(cache)
     sums = in_vmem(lax.all_to_all(spread, "zz", 0, 0, tiled=True))
+    width = GROUP * HS
+    group_cols = pl.BlockSpec((block, width), lambda h: (0, h))
+    head_cols = pl.BlockSpec((block, HS), lambda h: (0, h))
+    group_heads = pl.BlockSpec((GROUP, HS, block), lambda h: (h, 0, 0))
+    group_stats = pl.BlockSpec((GROUP, 2, block), lambda h: (h, 0, 0))
+    with jax.named_scope("own"):
+        own, own_stats = pl.pallas_call(
+            own_kernel,
+            out_shape=(shape((HQ, HS, block), F32), shape((HQ, 2, block), F32)),
+            name="own",
+            grid=(HK,),
+            in_specs=[group_cols, head_cols, head_cols],
+            out_specs=[group_heads, group_stats],
+            interpret=INTERPRET,
+        )(ctx_query, ctx_key, ctx_value)
     parts, new = call(
         decode_kernel,
         (shape((far, QROWS + SROWS + piece, HS), BF16), shape((3, QROWS, HS), F32)),
@@ -310,19 +350,18 @@
         in_specs=[VMEM_SPEC] * 2,
     )(parts, in_vmem(new))
     heads = in_vmem(lax.all_to_all(heads, ("x", "zo"), 0, 0, tiled=True))
-    width = GROUP * HS
     context_out, decoded = pl.pallas_call(
         prefill_kernel,
         out_shape=(shape((block, HQ * HS), BF16), shape((STEPS, HQ * HS), BF16)),
         name="prefill",
         grid=(HK,),
-        in_specs=[VMEM_SPEC] * 4,
+        in_specs=[group_cols, group_heads, group_stats, VMEM_SPEC],
         out_specs=[
-            pl.BlockSpec((block, width), lambda h: (0, h)),
+            group_cols,
             pl.BlockSpec((STEPS, width), lambda h: (0, h)),
         ],
         interpret=INTERPRET,
-    )(in_vmem(ctx_query), in_vmem(ctx_key), in_vmem(ctx_value), heads)
+    )(ctx_query, own, own_stats, heads)
     return context_out, decoded
 
 

time: 88.3 us -> 86.3 us (0.977)
  blocking collectives: 46.4 us -> 33.9 us
  Pallas kernels: 12 us -> 15.8 us
  starting transfers between devices: 14.2 us -> 17.7 us
  waiting for transfers between devices: 14.6 us -> 17.6 us
    all_to_all x1 -> x0, blocking collectives: 12.3 us -> none  [on_device(): heads = in_vmem(lax.all_to_all(heads, ('x', 'zo'), 0, 0, tiled=True))]
    pallas_call x0 -> x1, Pallas kernels: none -> 6.27 us  [on_device(): pl.pallas_call(own_kernel, out_shape=(shape((HQ, HS, block), F32), shape(...]
    all_to_all x0 -> x1, starting transfers between devices: none -> 3.54 us  [on_device(): heads = in_vmem(lax.all_to_all(heads, ('x', 'zo'), 0, 0, tiled=True))]
    all_to_all x0 -> x1, waiting for transfers between devices: none -> 2.96 us  [on_device(): heads = in_vmem(lax.all_to_all(heads, ('x', 'zo'), 0, 0, tiled=True))]
    pallas_call x1, Pallas kernels: 7.19 us -> 5.24 us  [on_device(): pl.pallas_call(prefill_kernel, out_shape=(shape((block, HQ * HS), BF16),...]
    pallas_call x1, Pallas kernels: 2.23 us -> 0.88 us  [on_device(): call(decode_kernel, (shape((far, QROWS + SROWS + piece, HS), BF16), shape...]
  transfers between devices with their start and end apart: 1 -> 2, of which waited for: 1 -> 2; matrix products, arithmetic and copies ran while one was open for 0% -> 0% of each run, Pallas kernels for 0% -> 7%
where the time goes in v4:
time: 86.3 us; the launch traced here: 85.8 us
  blocking collectives  33.9 us (39%)
  starting transfers between devices  17.7 us (21%)
  waiting for transfers between devices  17.6 us (20%)
  Pallas kernels  15.8 us (18%)
    all_to_all x1, blocking collectives, on_device(): parts = in_vmem(lax.all_to_all(parts, 'zz', 0, 0, tiled=True))  17.2 us
    all_to_all x1, blocking collectives, on_device(): cache = in_vmem(lax.all_to_all(slabs, ('x', 'zo'), 0, 0, tiled=True))  16.7 us
    all_to_all x1, waiting for transfers between devices, on_device(): sums = in_vmem(lax.all_to_all(spread, 'zz', 0, 0, tiled=True))  14.6 us
    all_to_all x1, starting transfers between devices, on_device(): sums = in_vmem(lax.all_to_all(spread, 'zz', 0, 0, tiled=True))  14.2 us
    pallas_call x1, Pallas kernels, on_device(): pl.pallas_call(own_kernel, out_shape=(shape((HQ, HS, block), F32), shape(...  6.27 us
    pallas_call x1, Pallas kernels, on_device(): pl.pallas_call(prefill_kernel, out_shape=(shape((block, HQ * HS), BF16),...  5.24 us
    all_to_all x1, starting transfers between devices, on_device(): heads = in_vmem(lax.all_to_all(heads, ('x', 'zo'), 0, 0, tiled=True))  3.54 us
    all_to_all x1, waiting for transfers between devices, on_device(): heads = in_vmem(lax.all_to_all(heads, ('x', 'zo'), 0, 0, tiled=True))  2.96 us
  transfers between devices with their start and end apart: 2, of which 2 were waited for; matrix products, arithmetic and copies ran while one was open for 0% of the time, Pallas kernels for 7%

profile of v4, /device:TPU:24, one launch (start us, length us, event | category | flops | bytes accessed | tf_op | source)
XLA Modules:
  0.0 85.8 jit_solution(1292109927220883207)
XLA Ops:
  0.6 1.5 %project.1 = bf16[8,304,128]{2,1,0:T(8,128)(2,1)S(1)} custom-call(bf16[4,64]{1,0:T(4,128)(2,1)} %embed_ref.1, bf16[64,2048]{1,0:T(8,128)(2,1)} %wq_ref.1, bf16[64,512]{1,0:T(8,128)(2,1)} %wk_ref.1, bf16[64,512]{1,0:T(8,128)(2,1)} %wv_ref.1, bf16[256,512]{1,0:T(8,128)(2,1)} %key_ref.3, bf16[256,512]{1,0:T(8,128)(2,1)} %value_ref.3), custom_call_target="tpu_custom_call" | custom-call | tf_op jit(solution)/shard_map/project/pallas_call | solution.py:310
  2.1 16.7 %all_to_all.20.in_ref.cache_ref = bf16[8,304,128]{2,1,0:T(8,128)(2,1)S(1)} all-to-all(bf16[8,304,128]{2,1,0:T(8,128)(2,1)S(1)} %project.1), channel_id=1, replica_groups=mesh['doc'=8,'x'=4,'zz'=8,'zo'=2] {'x','zo'}, dimensions={0} | all-to-all | bytes 1245184 | tf_op jit(solution)/shard_map/all_to_all | solution.py:316
  18.8 0.7 spread.1
  19.5 14.2 %all-to-all-start.1 = ((bf16[8,80,128]{2,1,0:T(8,128)(2,1)}), bf16[8,80,128]{2,1,0:T(8,128)(2,1)S(1)}, u32[]{:S(2)}, u32[]{:S(2)}) async-start(bf16[8,80,128]{2,1,0:T(8,128)(2,1)} %spread.1), calls=%async_computation.1 | async-start | bytes 327680 | tf_op jit(solution)/shard_map/all_to_all | solution.py:323
  33.8 0.1 negate_select_fusion
  33.9 14.6 %all-to-all-done.1.sums_ref = bf16[8,80,128]{2,1,0:T(8,128)(2,1)S(1)} async-done(((bf16[8,80,128]{2,1,0:T(8,128)(2,1)}), bf16[8,80,128]{2,1,0:T(8,128)(2,1)S(1)}, u32[]{:S(2)}, u32[]{:S(2)}) %all-to-all-start.1) | async-done | bytes 163872 | tf_op jit(solution)/shard_map/all_to_all | solution.py:323
  48.5 0.9 %decode.1 = (bf16[8,56,128]{2,1,0:T(8,128)(2,1)S(1)}, f32[3,16,128]{2,1,0:T(8,128)S(1)}) custom-call(bf16[8,80,128]{2,1,0:T(8,128)(2,1)S(1)} %all-to-all-done.1.sums_ref, bf16[8,304,128]{2,1,0:T(8,128)(2,1)S(1)} %all_to_all.20.in_ref.cache_ref, f32[24,128]{1,0:T(8,128)S(1)} %get-tuple-element.11.cos_ref, f32[24,128]{1,0:T(8,128)S(1)} %get-tuple-element.10.sin_ref), custom_call_target="tpu_custom_call" | custom-call | tf_op jit(solution)/shard_map/decode/pallas_call | solution.py:339
  49.4 17.2 %all_to_all.21.parts_ref = bf16[8,56,128]{2,1,0:T(8,128)(2,1)S(1)} all-to-all(bf16[8,56,128]{2,1,0:T(8,128)(2,1)S(1)} %get-tuple-element.8), channel_id=1, replica_groups=mesh['doc'=8,'x'=4,'zz'=8,'zo'=2] {'zz'}, dimensions={0} | all-to-all | bytes 229376 | tf_op jit(solution)/shard_map/all_to_all | solution.py:345
  66.6 1.2 %combine.1 = bf16[8,296,128]{2,1,0:T(8,128)(2,1)} custom-call(bf16[8,56,128]{2,1,0:T(8,128)(2,1)S(1)} %all_to_all.21.parts_ref, f32[3,16,128]{2,1,0:T(8,128)S(1)} %get-tuple-element.9.new_ref), custom_call_target="tpu_custom_call" | custom-call | tf_op jit(solution)/shard_map/combine/pallas_call | solution.py:346
  67.8 3.5 %all-to-all-start.3 = ((bf16[8,296,128]{2,1,0:T(8,128)(2,1)}), bf16[8,296,128]{2,1,0:T(8,128)(2,1)S(1)}, u32[]{:S(2)}, u32[]{:S(2)}) async-start(bf16[8,296,128]{2,1,0:T(8,128)(2,1)} %combine.1), calls=%async_computation.3 | async-start | bytes 1212416 | tf_op jit(solution)/shard_map/all_to_all | solution.py:352
  71.4 6.3 %own.1 = (f32[16,128,256]{2,1,0:T(8,128)}, f32[16,2,256]{2,1,0:T(2,128)}) custom-call(bf16[256,2048]{1,0:T(8,128)(2,1)} %query_ref.3, bf16[256,512]{1,0:T(8,128)(2,1)} %key_ref.3, bf16[256,512]{1,0:T(8,128)(2,1)} %value_ref.3), custom_call_target="tpu_custom_call" | custom-call | tf_op jit(solution)/shard_map/own/own/pallas_call | solution.py:330
  77.6 3.0 %all-to-all-done.3.anchor_ref = bf16[8,296,128]{2,1,0:T(8,128)(2,1)S(1)} async-done(((bf16[8,296,128]{2,1,0:T(8,128)(2,1)}), bf16[8,296,128]{2,1,0:T(8,128)(2,1)S(1)}, u32[]{:S(2)}, u32[]{:S(2)}) %all-to-all-start.3) | async-done | bytes 606240 | tf_op jit(solution)/shard_map/all_to_all | solution.py:352
  80.6 5.2 %prefill.1 = (bf16[256,2048]{1,0:T(8,128)(2,1)}, bf16[4,2048]{1,0:T(4,128)(2,1)}) custom-call(bf16[256,2048]{1,0:T(8,128)(2,1)} %query_ref.3, f32[16,128,256]{2,1,0:T(8,128)} %get-tuple-element.6.own_ref, f32[16,2,256]{2,1,0:T(2,128)} %get-tuple-element.7.own_stats_ref, bf16[8,296,128]{2,1,0:T(8,128)(2,1)S(1)} %all-to-all-done.3.anchor_ref), custom_call_target="tpu_custom_call" | custom-call | tf_op jit(solution)/shard_map/prefill/pallas_call | solution.py:353
  (4 shorter events, 0.0 us)
Async XLA Ops:
  19.5 29.0 %all-to-all-start.1 = ((bf16[8,80,128]{2,1,0:T(8,128)(2,1)}), bf16[8,80,128]{2,1,0:T(8,128)(2,1)S(1)}, u32[]{:S(2)}, u32[]{:S(2)}) async-start(bf16[8,80,128]{2,1,0:T(8,128)(2,1)} %spread.1), calls=%async_computation.1 | async-start | bytes 327680 | tf_op jit(solution)/shard_map/all_to_all | solution.py:323
  67.8 12.8 %all-to-all-start.3 = ((bf16[8,296,128]{2,1,0:T(8,128)(2,1)}), bf16[8,296,128]{2,1,0:T(8,128)(2,1)S(1)}, u32[]{:S(2)}, u32[]{:S(2)}) async-start(bf16[8,296,128]{2,1,0:T(8,128)(2,1)} %combine.1), calls=%async_computation.3 | async-start | bytes 1212416 | tf_op jit(solution)/shard_map/all_to_all | solution.py:352

commit v5 on v4

--- a/solution.py
+++ b/solution.py
@@ -8,6 +8,7 @@
 from jax.experimental.pallas import tpu as pltpu
 from jax.sharding import Mesh
 from jax.sharding import PartitionSpec as P
+
 
 HS = 128
 HQ = 16
@@ -198,6 +199,7 @@
         jnp.int32, (half, half), 1
     )
     for j in range(GROUP):
+        head = pl.program_id(0) * GROUP + j
         query = query_ref[:, j * HS : (j + 1) * HS]
         early = dot_t(key[:half], query)
         late = dot_t(key[half:], query[half:])
@@ -210,9 +212,10 @@
                 scores = jnp.concatenate([early[:, rows], late], axis=0)
             own_max = jnp.max(scores, axis=0, keepdims=True)
             weights = jnp.exp2((scores - own_max) * EXP2_SCALE)
-            stats_ref[j, 0:1, rows] = own_max
-            stats_ref[j, 1:2, rows] = jnp.sum(weights, axis=0, keepdims=True)
-            out_ref[j, :, rows] = dot(values[:, : (part + 1) * half], weights.astype(BF16))
+            stats_ref[head, 0:1, rows] = own_max
+            stats_ref[head, 1:2, rows] = jnp.sum(weights, axis=0, keepdims=True)
+            weighted = dot(values[:, : (part + 1) * half], weights.astype(BF16))
+            out_ref[head, :, rows] = weighted.astype(BF16)
 
 
 def prefill_kernel(query_ref, own_ref, own_stats_ref, anchor_ref, out_ref, decoded_ref):
@@ -231,7 +234,8 @@
         return dot_t(keys, query_ref[rows, j * HS : (j + 1) * HS])
 
     def weigh(scores, j, rows):
-        own_max, own_sum = own_stats_ref[j, 0:1, rows], own_stats_ref[j, 1:2, rows]
+        head = group * GROUP + j
+        own_max, own_sum = own_stats_ref[head, 0:1, rows], own_stats_ref[head, 1:2, rows]
         anchor_max = jnp.max(scores, axis=0, keepdims=True)
         row_max = jnp.where(use_anchor, jnp.maximum(own_max, anchor_max), own_max)
         shift = jnp.where(use_anchor, row_max, jnp.inf)
@@ -242,7 +246,8 @@
 
     def finish(weighed, j, rows):
         weights, own_factor, inverse = weighed
-        weighted = own_ref[j, :, rows] * own_factor + dot(values, weights)
+        own = own_ref[group * GROUP + j, :, rows].astype(F32)
+        weighted = own * own_factor + dot(values, weights)
         out_ref[rows, j * HS : (j + 1) * HS] = (weighted * inverse).T.astype(BF16)
 
     scores, weighed = scores_of(*units[0]), None
@@ -298,7 +303,7 @@
     )
 
 
-def on_device(ctx_query, ctx_key, ctx_value, step_embed, w_query, w_key, w_value):
+def layer(ctx_query, ctx_key, ctx_value, step_embed, w_query, w_key, w_value):
     block = ctx_query.shape[0]
     parities, far = lax.axis_size("zo"), lax.axis_size("zz")
     near = lax.axis_size("x") * parities
@@ -320,22 +325,18 @@
         name="spread",
         in_specs=[VMEM_SPEC],
     )(cache)
-    sums = in_vmem(lax.all_to_all(spread, "zz", 0, 0, tiled=True))
+    sums = lax.all_to_all(spread, "zz", 0, 0, tiled=True)
+    sums = in_vmem(sums)
     width = GROUP * HS
     group_cols = pl.BlockSpec((block, width), lambda h: (0, h))
     head_cols = pl.BlockSpec((block, HS), lambda h: (0, h))
-    group_heads = pl.BlockSpec((GROUP, HS, block), lambda h: (h, 0, 0))
-    group_stats = pl.BlockSpec((GROUP, 2, block), lambda h: (h, 0, 0))
-    with jax.named_scope("own"):
-        own, own_stats = pl.pallas_call(
-            own_kernel,
-            out_shape=(shape((HQ, HS, block), F32), shape((HQ, 2, block), F32)),
-            name="own",
-            grid=(HK,),
-            in_specs=[group_cols, head_cols, head_cols],
-            out_specs=[group_heads, group_stats],
-            interpret=INTERPRET,
-        )(ctx_query, ctx_key, ctx_value)
+    own, own_stats = call(
+        own_kernel,
+        (shape((HQ, HS, block), BF16), shape((HQ, 2, block), F32)),
+        name="own",
+        grid=(HK,),
+        in_specs=[group_cols, head_cols, head_cols],
+    )(ctx_query, ctx_key, ctx_value)
     parts, new = call(
         decode_kernel,
         (shape((far, QROWS + SROWS + piece, HS), BF16), shape((3, QROWS, HS), F32)),
@@ -355,13 +356,13 @@
         out_shape=(shape((block, HQ * HS), BF16), shape((STEPS, HQ * HS), BF16)),
         name="prefill",
         grid=(HK,),
-        in_specs=[group_cols, group_heads, group_stats, VMEM_SPEC],
+        in_specs=[group_cols] + [VMEM_SPEC] * 3,
         out_specs=[
             group_cols,
             pl.BlockSpec((STEPS, width), lambda h: (0, h)),
         ],
         interpret=INTERPRET,
-    )(ctx_query, own, own_stats, heads)
+    )(ctx_query, in_vmem(own), in_vmem(own_stats), heads)
     return context_out, decoded
 
 
@@ -371,7 +372,7 @@
     ctx = ("x", "zz", "zo")
     rows = P(("doc",) + ctx, None)
     return jax.shard_map(
-        on_device,
+        layer,
         mesh=split,
         in_specs=(rows, rows, rows, P("doc", ctx), P(ctx, None), P(ctx, None), P(ctx, None)),
         out_specs=(rows, P("doc", None)),

time: 86.3 us -> 85.9 us (level)
  Pallas kernels: 15.8 us -> 14.5 us
    pallas_call x6, Pallas kernels: 15.8 us -> 14.5 us  [the longest x1 5.39 us: layer(): call(own_kernel, (shape((HQ, HS, block), BF16), shape((HQ, 2, block), F32...]
    all_to_all x2, waiting for transfers between devices: 17.6 us -> 18.4 us  [the longest x1 14.6 us: layer(): sums = lax.all_to_all(spread, 'zz', 0, 0, tiled=True)]
  transfers between devices with their start and end apart: 2 -> 2, of which waited for: 2 -> 2; matrix products, arithmetic and copies ran while one was open for 0% -> 0% of each run, Pallas kernels for 7% -> 6%
where the time goes in v5:
time: 85.9 us; the launch traced here: 85.5 us
  blocking collectives  33.9 us (39%)
  waiting for transfers between devices  18.4 us (21%)
  starting transfers between devices  17.7 us (21%)
  Pallas kernels  14.5 us (17%)
    all_to_all x1, blocking collectives, layer(): parts = in_vmem(lax.all_to_all(parts, 'zz', 0, 0, tiled=True))  17.2 us
    all_to_all x1, blocking collectives, layer(): cache = in_vmem(lax.all_to_all(slabs, ('x', 'zo'), 0, 0, tiled=True))  16.7 us
    all_to_all x1, waiting for transfers between devices, layer(): sums = lax.all_to_all(spread, 'zz', 0, 0, tiled=True)  14.6 us
    all_to_all x1, starting transfers between devices, layer(): sums = lax.all_to_all(spread, 'zz', 0, 0, tiled=True)  14.2 us
    pallas_call x1, Pallas kernels, layer(): call(own_kernel, (shape((HQ, HS, block), BF16), shape((HQ, 2, block), F32...  5.39 us
    pallas_call x1, Pallas kernels, layer(): pl.pallas_call(prefill_kernel, out_shape=(shape((block, HQ * HS), BF16),...  4.88 us
    all_to_all x1, waiting for transfers between devices, layer(): heads = in_vmem(lax.all_to_all(heads, ('x', 'zo'), 0, 0, tiled=True))  3.83 us
    all_to_all x1, starting transfers between devices, layer(): heads = in_vmem(lax.all_to_all(heads, ('x', 'zo'), 0, 0, tiled=True))  3.54 us
  transfers between devices with their start and end apart: 2, of which 2 were waited for; matrix products, arithmetic and copies ran while one was open for 0% of the time, Pallas kernels for 6%

profile of v5, /device:TPU:24, one launch (start us, length us, event | category | flops | bytes accessed | tf_op | source)
XLA Modules:
  0.0 85.5 jit_solution(3606542427417860378)
XLA Ops:
  0.6 1.5 %project.1 = bf16[8,304,128]{2,1,0:T(8,128)(2,1)S(1)} custom-call(bf16[4,64]{1,0:T(4,128)(2,1)} %embed_ref.1, bf16[64,2048]{1,0:T(8,128)(2,1)} %wq_ref.1, bf16[64,512]{1,0:T(8,128)(2,1)} %wk_ref.1, bf16[64,512]{1,0:T(8,128)(2,1)} %wv_ref.1, bf16[256,512]{1,0:T(8,128)(2,1)} %key_ref.3, bf16[256,512]{1,0:T(8,128)(2,1)} %value_ref.3), custom_call_target="tpu_custom_call" | custom-call | tf_op jit(solution)/shard_map/project/pallas_call | solution.py:315
  2.1 16.7 %all_to_all.20.in_ref.cache_ref = bf16[8,304,128]{2,1,0:T(8,128)(2,1)S(1)} all-to-all(bf16[8,304,128]{2,1,0:T(8,128)(2,1)S(1)} %project.1), channel_id=1, replica_groups=mesh['doc'=8,'x'=4,'zz'=8,'zo'=2] {'x','zo'}, dimensions={0} | all-to-all | bytes 1245184 | tf_op jit(solution)/shard_map/all_to_all | solution.py:321
  18.8 0.7 spread.1
  19.5 14.2 %all-to-all-start.1 = ((bf16[8,80,128]{2,1,0:T(8,128)(2,1)}), bf16[8,80,128]{2,1,0:T(8,128)(2,1)S(1)}, u32[]{:S(2)}, u32[]{:S(2)}) async-start(bf16[8,80,128]{2,1,0:T(8,128)(2,1)} %spread.1), calls=%async_computation.1 | async-start | bytes 327680 | tf_op jit(solution)/shard_map/all_to_all | solution.py:328
  33.8 0.1 negate_select_fusion
  33.9 14.6 %all-to-all-done.1.sums_ref = bf16[8,80,128]{2,1,0:T(8,128)(2,1)S(1)} async-done(((bf16[8,80,128]{2,1,0:T(8,128)(2,1)}), bf16[8,80,128]{2,1,0:T(8,128)(2,1)S(1)}, u32[]{:S(2)}, u32[]{:S(2)}) %all-to-all-start.1) | async-done | bytes 163872 | tf_op jit(solution)/shard_map/all_to_all | solution.py:328
  48.5 0.9 %decode.1 = (bf16[8,56,128]{2,1,0:T(8,128)(2,1)S(1)}, f32[3,16,128]{2,1,0:T(8,128)S(1)}) custom-call(bf16[8,80,128]{2,1,0:T(8,128)(2,1)S(1)} %all-to-all-done.1.sums_ref, bf16[8,304,128]{2,1,0:T(8,128)(2,1)S(1)} %all_to_all.20.in_ref.cache_ref, f32[24,128]{1,0:T(8,128)S(1)} %get-tuple-element.11.cos_ref, f32[24,128]{1,0:T(8,128)S(1)} %get-tuple-element.10.sin_ref), custom_call_target="tpu_custom_call" | custom-call | tf_op jit(solution)/shard_map/decode/pallas_call | solution.py:340
  49.4 17.2 %all_to_all.21.parts_ref = bf16[8,56,128]{2,1,0:T(8,128)(2,1)S(1)} all-to-all(bf16[8,56,128]{2,1,0:T(8,128)(2,1)S(1)} %get-tuple-element.8), channel_id=1, replica_groups=mesh['doc'=8,'x'=4,'zz'=8,'zo'=2] {'zz'}, dimensions={0} | all-to-all | bytes 229376 | tf_op jit(solution)/shard_map/all_to_all | solution.py:346
  66.6 1.2 %combine.1 = bf16[8,296,128]{2,1,0:T(8,128)(2,1)} custom-call(bf16[8,56,128]{2,1,0:T(8,128)(2,1)S(1)} %all_to_all.21.parts_ref, f32[3,16,128]{2,1,0:T(8,128)S(1)} %get-tuple-element.9.new_ref), custom_call_target="tpu_custom_call" | custom-call | tf_op jit(solution)/shard_map/combine/pallas_call | solution.py:347
  67.8 3.5 %all-to-all-start.3 = ((bf16[8,296,128]{2,1,0:T(8,128)(2,1)}), bf16[8,296,128]{2,1,0:T(8,128)(2,1)S(1)}, u32[]{:S(2)}, u32[]{:S(2)}) async-start(bf16[8,296,128]{2,1,0:T(8,128)(2,1)} %combine.1), calls=%async_computation.3 | async-start | bytes 1212416 | tf_op jit(solution)/shard_map/all_to_all | solution.py:353
  71.4 5.4 %own.1 = (bf16[16,128,256]{2,1,0:T(8,128)(2,1)S(1)}, f32[16,2,256]{2,1,0:T(2,128)S(1)}) custom-call(bf16[256,2048]{1,0:T(8,128)(2,1)} %query_ref.3, bf16[256,512]{1,0:T(8,128)(2,1)} %key_ref.3, bf16[256,512]{1,0:T(8,128)(2,1)} %value_ref.3), custom_call_target="tpu_custom_call" | custom-call | tf_op jit(solution)/shard_map/own/pallas_call | solution.py:333
  76.8 3.8 %all-to-all-done.3.anchor_ref = bf16[8,296,128]{2,1,0:T(8,128)(2,1)S(1)} async-done(((bf16[8,296,128]{2,1,0:T(8,128)(2,1)}), bf16[8,296,128]{2,1,0:T(8,128)(2,1)S(1)}, u32[]{:S(2)}, u32[]{:S(2)}) %all-to-all-start.3) | async-done | bytes 606240 | tf_op jit(solution)/shard_map/all_to_all | solution.py:353
  80.6 4.9 %prefill.1 = (bf16[256,2048]{1,0:T(8,128)(2,1)}, bf16[4,2048]{1,0:T(4,128)(2,1)}) custom-call(bf16[256,2048]{1,0:T(8,128)(2,1)} %query_ref.3, bf16[16,128,256]{2,1,0:T(8,128)(2,1)S(1)} %get-tuple-element.6.own_ref, f32[16,2,256]{2,1,0:T(2,128)S(1)} %get-tuple-element.7.own_stats_ref, bf16[8,296,128]{2,1,0:T(8,128)(2,1)S(1)} %all-to-all-done.3.anchor_ref), custom_call_target="tpu_custom_call" | custom-call | tf_op jit(solution)/shard_map/prefill/pallas_call | solution.py:354
  (4 shorter events, 0.0 us)
Async XLA Ops:
  19.5 29.0 %all-to-all-start.1 = ((bf16[8,80,128]{2,1,0:T(8,128)(2,1)}), bf16[8,80,128]{2,1,0:T(8,128)(2,1)S(1)}, u32[]{:S(2)}, u32[]{:S(2)}) async-start(bf16[8,80,128]{2,1,0:T(8,128)(2,1)} %spread.1), calls=%async_computation.1 | async-start | bytes 327680 | tf_op jit(solution)/shard_map/all_to_all | solution.py:328
  67.8 12.8 %all-to-all-start.3 = ((bf16[8,296,128]{2,1,0:T(8,128)(2,1)}), bf16[8,296,128]{2,1,0:T(8,128)(2,1)S(1)}, u32[]{:S(2)}, u32[]{:S(2)}) async-start(bf16[8,296,128]{2,1,0:T(8,128)(2,1)} %combine.1), calls=%async_computation.3 | async-start | bytes 1212416 | tf_op jit(solution)/shard_map/all_to_all | solution.py:353

commit v6 on v5

--- a/solution.py
+++ b/solution.py
@@ -143,7 +143,7 @@
     )
     stats = pack_stats(joint_max, joint_sum)
     joint_out = joint_out.astype(BF16)
-    anchor = sums_ref[0, 2 * PROWS : 2 * PROWS + piece]
+    anchor = sums_ref[peers // 2, 2 * PROWS : 2 * PROWS + piece]
     for peer in range(peers):
         out_ref[peer, 0:QROWS] = joint_out
         out_ref[peer, QROWS : QROWS + SROWS] = stats
@@ -303,6 +303,12 @@
     )
 
 
+def exchange_far(value):
+    far = lax.axis_size("zz")
+    order = [(at + far // 2) % far for at in range(far)]
+    return lax.all_to_all(value, "zz", 0, 0, axis_index_groups=[order], tiled=True)
+
+
 def layer(ctx_query, ctx_key, ctx_value, step_embed, w_query, w_key, w_value):
     block = ctx_query.shape[0]
     parities, far = lax.axis_size("zo"), lax.axis_size("zz")
@@ -325,7 +331,7 @@
         name="spread",
         in_specs=[VMEM_SPEC],
     )(cache)
-    sums = lax.all_to_all(spread, "zz", 0, 0, tiled=True)
+    sums = exchange_far(spread)
     sums = in_vmem(sums)
     width = GROUP * HS
     group_cols = pl.BlockSpec((block, width), lambda h: (0, h))
@@ -343,7 +349,7 @@
         name="decode",
         in_specs=[VMEM_SPEC] * 4,
     )(sums, cache, in_vmem(cosine), in_vmem(sine))
-    parts = in_vmem(lax.all_to_all(parts, "zz", 0, 0, tiled=True))
+    parts = in_vmem(exchange_far(parts))
     heads = call(
         combine_kernel,
         shape((near, HROWS + 2 * half, HS), BF16),

time: 85.9 us -> 79.8 us (0.929)
  waiting for transfers between devices: 18.4 us -> 9.21 us
  starting transfers between devices: 17.7 us -> 21 us
    all_to_all x1, waiting for transfers between devices: 14.6 us -> 5.54 us  [exchange_far(): lax.all_to_all(value, 'zz', 0, 0, axis_index_groups=[order], tiled=True)]
    all_to_all x1, starting transfers between devices: 14.2 us -> 17.5 us  [exchange_far(): lax.all_to_all(value, 'zz', 0, 0, axis_index_groups=[order], tiled=True)]
  transfers between devices with their start and end apart: 2 -> 2, of which waited for: 2 -> 2; matrix products, arithmetic and copies ran while one was open for 0% -> 0% of each run, Pallas kernels for 6% -> 7%
where the time goes in v6:
time: 79.8 us; the launch traced here: 79.3 us
  blocking collectives  33.8 us (42%)
  starting transfers between devices  21 us (26%)
  Pallas kernels  14.5 us (18%)
  waiting for transfers between devices  9.21 us (12%)
    all_to_all x1, starting transfers between devices, exchange_far(): lax.all_to_all(value, 'zz', 0, 0, axis_index_groups=[order], tiled=True)  17.5 us
    all_to_all x1, blocking collectives, exchange_far(): lax.all_to_all(value, 'zz', 0, 0, axis_index_groups=[order], tiled=True)  17 us
    all_to_all x1, blocking collectives, layer(): cache = in_vmem(lax.all_to_all(slabs, ('x', 'zo'), 0, 0, tiled=True))  16.7 us
    all_to_all x1, waiting for transfers between devices, exchange_far(): lax.all_to_all(value, 'zz', 0, 0, axis_index_groups=[order], tiled=True)  5.54 us
    pallas_call x1, Pallas kernels, layer(): call(own_kernel, (shape((HQ, HS, block), BF16), shape((HQ, 2, block), F32...  5.39 us
    pallas_call x1, Pallas kernels, layer(): pl.pallas_call(prefill_kernel, out_shape=(shape((block, HQ * HS), BF16),...  4.87 us
    all_to_all x1, waiting for transfers between devices, layer(): heads = in_vmem(lax.all_to_all(heads, ('x', 'zo'), 0, 0, tiled=True))  3.66 us
    all_to_all x1, starting transfers between devices, layer(): heads = in_vmem(lax.all_to_all(heads, ('x', 'zo'), 0, 0, tiled=True))  3.54 us
  transfers between devices with their start and end apart: 2, of which 2 were waited for; matrix products, arithmetic and copies ran while one was open for 0% of the time, Pallas kernels for 7%

profile of v6, /device:TPU:24, one launch (start us, length us, event | category | flops | bytes accessed | tf_op | source)
XLA Modules:
  0.0 79.3 jit_solution(15093450695127274712)
XLA Ops:
  0.6 1.5 %project.1 = bf16[8,304,128]{2,1,0:T(8,128)(2,1)S(1)} custom-call(bf16[4,64]{1,0:T(4,128)(2,1)} %embed_ref.1, bf16[64,2048]{1,0:T(8,128)(2,1)} %wq_ref.1, bf16[64,512]{1,0:T(8,128)(2,1)} %wk_ref.1, bf16[64,512]{1,0:T(8,128)(2,1)} %wv_ref.1, bf16[256,512]{1,0:T(8,128)(2,1)} %key_ref.3, bf16[256,512]{1,0:T(8,128)(2,1)} %value_ref.3), custom_call_target="tpu_custom_call" | custom-call | tf_op jit(solution)/shard_map/project/pallas_call | solution.py:321
  2.1 16.7 %all_to_all.20.in_ref.cache_ref = bf16[8,304,128]{2,1,0:T(8,128)(2,1)S(1)} all-to-all(bf16[8,304,128]{2,1,0:T(8,128)(2,1)S(1)} %project.1), channel_id=1, replica_groups=mesh['doc'=8,'x'=4,'zz'=8,'zo'=2] {'x','zo'}, dimensions={0} | all-to-all | bytes 1245184 | tf_op jit(solution)/shard_map/all_to_all | solution.py:327
  18.8 0.7 spread.1
  19.5 17.5 %all-to-all-start.1 = ((bf16[8,80,128]{2,1,0:T(8,128)(2,1)}), bf16[8,80,128]{2,1,0:T(8,128)(2,1)S(1)}, u32[]{:S(2)}, u32[]{:S(2)}) async-start(bf16[8,80,128]{2,1,0:T(8,128)(2,1)} %spread.1), calls=%async_computation.1 | async-start | bytes 327680 | tf_op jit(solution)/shard_map/all_to_all | solution.py:309
  37.0 0.1 negate_select_fusion
  37.2 5.5 %all-to-all-done.1.sums_ref = bf16[8,80,128]{2,1,0:T(8,128)(2,1)S(1)} async-done(((bf16[8,80,128]{2,1,0:T(8,128)(2,1)}), bf16[8,80,128]{2,1,0:T(8,128)(2,1)S(1)}, u32[]{:S(2)}, u32[]{:S(2)}) %all-to-all-start.1) | async-done | bytes 163872 | tf_op jit(solution)/shard_map/all_to_all | solution.py:309
  42.7 0.9 %decode.1 = (bf16[8,56,128]{2,1,0:T(8,128)(2,1)S(1)}, f32[3,16,128]{2,1,0:T(8,128)S(1)}) custom-call(bf16[8,80,128]{2,1,0:T(8,128)(2,1)S(1)} %all-to-all-done.1.sums_ref, bf16[8,304,128]{2,1,0:T(8,128)(2,1)S(1)} %all_to_all.20.in_ref.cache_ref, f32[24,128]{1,0:T(8,128)S(1)} %get-tuple-element.11.cos_ref, f32[24,128]{1,0:T(8,128)S(1)} %get-tuple-element.10.sin_ref), custom_call_target="tpu_custom_call" | custom-call | tf_op jit(solution)/shard_map/decode/pallas_call | solution.py:346
  43.6 17.0 %all_to_all.21.parts_ref = bf16[8,56,128]{2,1,0:T(8,128)(2,1)S(1)} all-to-all(bf16[8,56,128]{2,1,0:T(8,128)(2,1)S(1)} %get-tuple-element.8), channel_id=1, replica_groups={{8,10,12,14,0,2,4,6},{9,11,13,15,1,3,5,7},{24,26,28,30,16,18,20,22},{25..., dimensions={0} | all-to-all | bytes 229376 | tf_op jit(solution)/shard_map/all_to_all | solution.py:309
  60.6 1.2 %combine.1 = bf16[8,296,128]{2,1,0:T(8,128)(2,1)} custom-call(bf16[8,56,128]{2,1,0:T(8,128)(2,1)S(1)} %all_to_all.21.parts_ref, f32[3,16,128]{2,1,0:T(8,128)S(1)} %get-tuple-element.9.new_ref), custom_call_target="tpu_custom_call" | custom-call | tf_op jit(solution)/shard_map/combine/pallas_call | solution.py:353
  61.8 3.5 %all-to-all-start.3 = ((bf16[8,296,128]{2,1,0:T(8,128)(2,1)}), bf16[8,296,128]{2,1,0:T(8,128)(2,1)S(1)}, u32[]{:S(2)}, u32[]{:S(2)}) async-start(bf16[8,296,128]{2,1,0:T(8,128)(2,1)} %combine.1), calls=%async_computation.3 | async-start | bytes 1212416 | tf_op jit(solution)/shard_map/all_to_all | solution.py:359
  65.4 5.4 %own.1 = (bf16[16,128,256]{2,1,0:T(8,128)(2,1)S(1)}, f32[16,2,256]{2,1,0:T(2,128)S(1)}) custom-call(bf16[256,2048]{1,0:T(8,128)(2,1)} %query_ref.3, bf16[256,512]{1,0:T(8,128)(2,1)} %key_ref.3, bf16[256,512]{1,0:T(8,128)(2,1)} %value_ref.3), custom_call_target="tpu_custom_call" | custom-call | tf_op jit(solution)/shard_map/own/pallas_call | solution.py:339
  70.8 3.7 %all-to-all-done.3.anchor_ref = bf16[8,296,128]{2,1,0:T(8,128)(2,1)S(1)} async-done(((bf16[8,296,128]{2,1,0:T(8,128)(2,1)}), bf16[8,296,128]{2,1,0:T(8,128)(2,1)S(1)}, u32[]{:S(2)}, u32[]{:S(2)}) %all-to-all-start.3) | async-done | bytes 606240 | tf_op jit(solution)/shard_map/all_to_all | solution.py:359
  74.5 4.9 %prefill.1 = (bf16[256,2048]{1,0:T(8,128)(2,1)}, bf16[4,2048]{1,0:T(4,128)(2,1)}) custom-call(bf16[256,2048]{1,0:T(8,128)(2,1)} %query_ref.3, bf16[16,128,256]{2,1,0:T(8,128)(2,1)S(1)} %get-tuple-element.6.own_ref, f32[16,2,256]{2,1,0:T(2,128)S(1)} %get-tuple-element.7.own_stats_ref, bf16[8,296,128]{2,1,0:T(8,128)(2,1)S(1)} %all-to-all-done.3.anchor_ref), custom_call_target="tpu_custom_call" | custom-call | tf_op jit(solution)/shard_map/prefill/pallas_call | solution.py:360
  (4 shorter events, 0.0 us)
Async XLA Ops:
  19.5 23.2 %all-to-all-start.1 = ((bf16[8,80,128]{2,1,0:T(8,128)(2,1)}), bf16[8,80,128]{2,1,0:T(8,128)(2,1)S(1)}, u32[]{:S(2)}, u32[]{:S(2)}) async-start(bf16[8,80,128]{2,1,0:T(8,128)(2,1)} %spread.1), calls=%async_computation.1 | async-start | bytes 327680 | tf_op jit(solution)/shard_map/all_to_all | solution.py:309
  61.8 12.6 %all-to-all-start.3 = ((bf16[8,296,128]{2,1,0:T(8,128)(2,1)}), bf16[8,296,128]{2,1,0:T(8,128)(2,1)S(1)}, u32[]{:S(2)}, u32[]{:S(2)}) async-start(bf16[8,296,128]{2,1,0:T(8,128)(2,1)} %combine.1), calls=%async_computation.3 | async-start | bytes 1212416 | tf_op jit(solution)/shard_map/all_to_all | solution.py:359

commit v7 on v5

--- a/solution.py
+++ b/solution.py
@@ -6,7 +6,6 @@
 from jax import lax
 from jax.experimental import pallas as pl
 from jax.experimental.pallas import tpu as pltpu
-from jax.sharding import Mesh
 from jax.sharding import PartitionSpec as P
 
 
@@ -21,6 +20,8 @@
 HROWS = 2 * QROWS + SROWS
 SCALE = 1.0 / math.sqrt(HS)
 EXP2_SCALE = SCALE * math.log2(math.e)
+PARITIES = 2
+NEAR = HK * PARITIES
 BF16 = jnp.bfloat16
 F32 = jnp.float32
 INTERPRET = False
@@ -80,6 +81,7 @@
 
 
 def spread_kernel(in_ref, out_ref):
+    anchor = in_ref.shape[0] // 2
     peers = out_ref.shape[0]
     piece = out_ref.shape[1] - 2 * PROWS
     high, low = split2(add_projections(in_ref))
@@ -87,7 +89,7 @@
         out_ref[peer, 0:PROWS] = high
         out_ref[peer, PROWS : 2 * PROWS] = low
         start = 2 * PROWS + peer * piece
-        out_ref[peer, 2 * PROWS : 2 * PROWS + piece] = in_ref[0, start : start + piece]
+        out_ref[peer, 2 * PROWS : 2 * PROWS + piece] = in_ref[anchor, start : start + piece]
 
 
 def pack_stats(part_max, part_sum):
@@ -143,7 +145,7 @@
     )
     stats = pack_stats(joint_max, joint_sum)
     joint_out = joint_out.astype(BF16)
-    anchor = sums_ref[0, 2 * PROWS : 2 * PROWS + piece]
+    anchor = sums_ref[peers // 2, 2 * PROWS : 2 * PROWS + piece]
     for peer in range(peers):
         out_ref[peer, 0:QROWS] = joint_out
         out_ref[peer, QROWS : QROWS + SROWS] = stats
@@ -170,7 +172,7 @@
     for peer in range(peers):
         part_max, part_sum = unpack_stats(parts_ref[peer, QROWS:first])
         parts.append((part_max, part_sum, parts_ref[peer, 0:QROWS].astype(F32)))
-    has_new = lax.axis_index("zo") == 0
+    has_new = lax.axis_index("ctx") % PARITIES == 0
     new_max = new_ref[0][:, 0:1]
     parts.append(
         (
@@ -222,7 +224,7 @@
     group = pl.program_id(0)
     parities = anchor_ref.shape[0] // HK
     piece = (anchor_ref.shape[1] - HROWS) // 2
-    use_anchor = (lax.axis_index("x") + lax.axis_index("zz") + lax.axis_index("zo")) != 0
+    use_anchor = lax.axis_index("ctx") != 0
     near = [group * parities + parity for parity in range(parities)]
     keys = jnp.concatenate([anchor_ref[n, HROWS : HROWS + piece] for n in near], axis=0)
     values = jnp.concatenate([anchor_ref[n, HROWS + piece :] for n in near], axis=0).T
@@ -303,14 +305,31 @@
     )
 
 
+def groups_of(contexts):
+    far = contexts // NEAR
+
+    def index(x, zz, zo):
+        x, zz = (x + HK // 2) % HK, (zz + far // 2) % far
+        return (x * far + zz) * PARITIES + zo
+
+    xs, zzs, zos = range(HK), range(far), range(PARITIES)
+    near = [[index(x, zz, zo) for x in xs for zo in zos] for zz in zzs]
+    return near, [[index(x, zz, zo) for zz in zzs] for x in xs for zo in zos]
+
+
+def exchange(value, groups):
+    return lax.all_to_all(value, "ctx", 0, 0, axis_index_groups=groups, tiled=True)
+
+
 def layer(ctx_query, ctx_key, ctx_value, step_embed, w_query, w_key, w_value):
     block = ctx_query.shape[0]
-    parities, far = lax.axis_size("zo"), lax.axis_size("zz")
-    near = lax.axis_size("x") * parities
-    half = block // parities
+    contexts = lax.axis_size("ctx")
+    near, far = NEAR, contexts // NEAR
+    near_groups, far_groups = groups_of(contexts)
+    half = block // PARITIES
     piece = 2 * half // far
     shape = jax.ShapeDtypeStruct
-    cosine, sine = rotary_tables(near * far * block)
+    cosine, sine = rotary_tables(contexts * block)
 
     slabs = call(
         project_kernel,
@@ -318,14 +337,14 @@
         name="project",
         scratch_shapes=[pltpu.VMEM((HK, PROWS, HS), F32)],
     )(step_embed, w_query, w_key, w_value, ctx_key, ctx_value)
-    cache = in_vmem(lax.all_to_all(slabs, ("x", "zo"), 0, 0, tiled=True))
+    cache = in_vmem(exchange(slabs, near_groups))
     spread = call(
         spread_kernel,
         shape((far, 2 * PROWS + piece, HS), BF16),
         name="spread",
         in_specs=[VMEM_SPEC],
     )(cache)
-    sums = lax.all_to_all(spread, "zz", 0, 0, tiled=True)
+    sums = exchange(spread, far_groups)
     sums = in_vmem(sums)
     width = GROUP * HS
     group_cols = pl.BlockSpec((block, width), lambda h: (0, h))
@@ -343,14 +362,14 @@
         name="decode",
         in_specs=[VMEM_SPEC] * 4,
     )(sums, cache, in_vmem(cosine), in_vmem(sine))
-    parts = in_vmem(lax.all_to_all(parts, "zz", 0, 0, tiled=True))
+    parts = in_vmem(exchange(parts, far_groups))
     heads = call(
         combine_kernel,
         shape((near, HROWS + 2 * half, HS), BF16),
         name="combine",
         in_specs=[VMEM_SPEC] * 2,
     )(parts, in_vmem(new))
-    heads = in_vmem(lax.all_to_all(heads, ("x", "zo"), 0, 0, tiled=True))
+    heads = in_vmem(exchange(heads, near_groups))
     context_out, decoded = pl.pallas_call(
         prefill_kernel,
         out_shape=(shape((block, HQ * HS), BF16), shape((STEPS, HQ * HS), BF16)),
@@ -367,14 +386,11 @@
 
 
 def solution(mesh):
-    docs, contexts = mesh.shape["doc"], mesh.shape["ctx"]
-    split = Mesh(mesh.devices.reshape(docs, HK, contexts // (2 * HK), 2), ("doc", "x", "zz", "zo"))
-    ctx = ("x", "zz", "zo")
-    rows = P(("doc",) + ctx, None)
+    rows = P(("doc", "ctx"), None)
     return jax.shard_map(
         layer,
-        mesh=split,
-        in_specs=(rows, rows, rows, P("doc", ctx), P(ctx, None), P(ctx, None), P(ctx, None)),
+        mesh=mesh,
+        in_specs=(rows, rows, rows, P("doc", "ctx"), P("ctx", None), P("ctx", None), P("ctx", None)),
         out_specs=(rows, P("doc", None)),
         check_vma=False,
     )

time: 85.9 us -> 78.6 us (0.915)
  waiting for transfers between devices: 18.4 us -> 7.46 us
  starting transfers between devices: 17.7 us -> 24 us
  blocking collectives: 33.9 us -> 31.3 us
    all_to_all x2, waiting for transfers between devices: 18.4 us -> 7.46 us  [exchange(): lax.all_to_all(value, 'ctx', 0, 0, axis_index_groups=groups, tiled=True)]
    all_to_all x2, starting transfers between devices: 17.7 us -> 24 us  [exchange(): lax.all_to_all(value, 'ctx', 0, 0, axis_index_groups=groups, tiled=True)]
    all_to_all x2, blocking collectives: 33.9 us -> 31.3 us  [exchange(): lax.all_to_all(value, 'ctx', 0, 0, axis_index_groups=groups, tiled=True)]
  transfers between devices with their start and end apart: 2 -> 2, of which waited for: 2 -> 2; matrix products, arithmetic and copies ran while one was open for 0% -> 0% of each run, Pallas kernels for 6% -> 7%
where the time goes in v7:
time: 78.6 us; the launch traced here: 78.1 us
  blocking collectives  31.3 us (40%)
  starting transfers between devices  24 us (31%)
  Pallas kernels  14.5 us (18%)
  waiting for transfers between devices  7.46 us (9%)
    all_to_all x2, blocking collectives, exchange(): lax.all_to_all(value, 'ctx', 0, 0, axis_index_groups=groups, tiled=True)  31.3 us
    all_to_all x2, starting transfers between devices, exchange(): lax.all_to_all(value, 'ctx', 0, 0, axis_index_groups=groups, tiled=True)  24 us
    all_to_all x2, waiting for transfers between devices, exchange(): lax.all_to_all(value, 'ctx', 0, 0, axis_index_groups=groups, tiled=True)  7.46 us
    pallas_call x1, Pallas kernels, layer(): call(own_kernel, (shape((HQ, HS, block), BF16), shape((HQ, 2, block), F32...  5.38 us
    pallas_call x1, Pallas kernels, layer(): pl.pallas_call(prefill_kernel, out_shape=(shape((block, HQ * HS), BF16),...  4.88 us
  transfers between devices with their start and end apart: 2, of which 2 were waited for; matrix products, arithmetic and copies ran while one was open for 0% of the time, Pallas kernels for 7%

profile of v7, /device:TPU:24, one launch (start us, length us, event | category | flops | bytes accessed | tf_op | source)
XLA Modules:
  0.0 78.1 jit_solution(7668583410403651753)
XLA Ops:
  0.6 1.5 %project.1 = bf16[8,304,128]{2,1,0:T(8,128)(2,1)S(1)} custom-call(bf16[4,64]{1,0:T(4,128)(2,1)} %embed_ref.1, bf16[64,2048]{1,0:T(8,128)(2,1)} %wq_ref.1, bf16[64,512]{1,0:T(8,128)(2,1)} %wk_ref.1, bf16[64,512]{1,0:T(8,128)(2,1)} %wv_ref.1, bf16[256,512]{1,0:T(8,128)(2,1)} %key_ref.3, bf16[256,512]{1,0:T(8,128)(2,1)} %value_ref.3), custom_call_target="tpu_custom_call" | custom-call | tf_op jit(solution)/shard_map/project/pallas_call | solution.py:334
  2.1 15.2 %all_to_all.20.in_ref.cache_ref = bf16[8,304,128]{2,1,0:T(8,128)(2,1)S(1)} all-to-all(bf16[8,304,128]{2,1,0:T(8,128)(2,1)S(1)} %project.1), channel_id=1, replica_groups={{40,41,56,57,8,9,24,25},{42,43,58,59,10,11,26,27},{44,45,60,61,12,13,28..., dimensions={0} | all-to-all | bytes 1245184 | tf_op jit(solution)/shard_map/all_to_all | solution.py:321
  17.2 0.7 spread.1
  17.9 17.5 %all-to-all-start.1 = ((bf16[8,80,128]{2,1,0:T(8,128)(2,1)}), bf16[8,80,128]{2,1,0:T(8,128)(2,1)S(1)}, u32[]{:S(2)}, u32[]{:S(2)}) async-start(bf16[8,80,128]{2,1,0:T(8,128)(2,1)} %spread.1), calls=%async_computation.1 | async-start | bytes 327680 | tf_op jit(solution)/shard_map/all_to_all | solution.py:321
  35.5 0.1 negate_select_fusion
  35.6 6.4 %all-to-all-done.1.sums_ref = bf16[8,80,128]{2,1,0:T(8,128)(2,1)S(1)} async-done(((bf16[8,80,128]{2,1,0:T(8,128)(2,1)}), bf16[8,80,128]{2,1,0:T(8,128)(2,1)S(1)}, u32[]{:S(2)}, u32[]{:S(2)}) %all-to-all-start.1) | async-done | bytes 163872 | tf_op jit(solution)/shard_map/all_to_all | solution.py:321
  42.0 0.9 %decode.1 = (bf16[8,56,128]{2,1,0:T(8,128)(2,1)S(1)}, f32[3,16,128]{2,1,0:T(8,128)S(1)}) custom-call(bf16[8,80,128]{2,1,0:T(8,128)(2,1)S(1)} %all-to-all-done.1.sums_ref, bf16[8,304,128]{2,1,0:T(8,128)(2,1)S(1)} %all_to_all.20.in_ref.cache_ref, f32[24,128]{1,0:T(8,128)S(1)} %get-tuple-element.11.cos_ref, f32[24,128]{1,0:T(8,128)S(1)} %get-tuple-element.10.sin_ref), custom_call_target="tpu_custom_call" | custom-call | tf_op jit(solution)/shard_map/decode/pallas_call | solution.py:359
  42.9 16.2 %all_to_all.21.parts_ref = bf16[8,56,128]{2,1,0:T(8,128)(2,1)S(1)} all-to-all(bf16[8,56,128]{2,1,0:T(8,128)(2,1)S(1)} %get-tuple-element.8), channel_id=1, replica_groups={{40,42,44,46,32,34,36,38},{41,43,45,47,33,35,37,39},{56,58,60,62,48,50,..., dimensions={0} | all-to-all | bytes 229376 | tf_op jit(solution)/shard_map/all_to_all | solution.py:321
  59.0 1.2 %combine.1 = bf16[8,296,128]{2,1,0:T(8,128)(2,1)} custom-call(bf16[8,56,128]{2,1,0:T(8,128)(2,1)S(1)} %all_to_all.21.parts_ref, f32[3,16,128]{2,1,0:T(8,128)S(1)} %get-tuple-element.9.new_ref), custom_call_target="tpu_custom_call" | custom-call | tf_op jit(solution)/shard_map/combine/pallas_call | solution.py:366
  60.2 6.6 %all-to-all-start.3 = ((bf16[8,296,128]{2,1,0:T(8,128)(2,1)}), bf16[8,296,128]{2,1,0:T(8,128)(2,1)S(1)}, u32[]{:S(2)}, u32[]{:S(2)}) async-start(bf16[8,296,128]{2,1,0:T(8,128)(2,1)} %combine.1), calls=%async_computation.3 | async-start | bytes 1212416 | tf_op jit(solution)/shard_map/all_to_all | solution.py:321
  66.8 5.4 %own.1 = (bf16[16,128,256]{2,1,0:T(8,128)(2,1)S(1)}, f32[16,2,256]{2,1,0:T(2,128)S(1)}) custom-call(bf16[256,2048]{1,0:T(8,128)(2,1)} %query_ref.3, bf16[256,512]{1,0:T(8,128)(2,1)} %key_ref.3, bf16[256,512]{1,0:T(8,128)(2,1)} %value_ref.3), custom_call_target="tpu_custom_call" | custom-call | tf_op jit(solution)/shard_map/own/pallas_call | solution.py:352
  72.2 1.1 %all-to-all-done.3.anchor_ref = bf16[8,296,128]{2,1,0:T(8,128)(2,1)S(1)} async-done(((bf16[8,296,128]{2,1,0:T(8,128)(2,1)}), bf16[8,296,128]{2,1,0:T(8,128)(2,1)S(1)}, u32[]{:S(2)}, u32[]{:S(2)}) %all-to-all-start.3) | async-done | bytes 606240 | tf_op jit(solution)/shard_map/all_to_all | solution.py:321
  73.2 4.9 %prefill.1 = (bf16[256,2048]{1,0:T(8,128)(2,1)}, bf16[4,2048]{1,0:T(4,128)(2,1)}) custom-call(bf16[256,2048]{1,0:T(8,128)(2,1)} %query_ref.3, bf16[16,128,256]{2,1,0:T(8,128)(2,1)S(1)} %get-tuple-element.6.own_ref, f32[16,2,256]{2,1,0:T(2,128)S(1)} %get-tuple-element.7.own_stats_ref, bf16[8,296,128]{2,1,0:T(8,128)(2,1)S(1)} %all-to-all-done.3.anchor_ref), custom_call_target="tpu_custom_call" | custom-call | tf_op jit(solution)/shard_map/prefill/pallas_call | solution.py:373
  (4 shorter events, 0.0 us)
Async XLA Ops:
  17.9 24.0 %all-to-all-start.1 = ((bf16[8,80,128]{2,1,0:T(8,128)(2,1)}), bf16[8,80,128]{2,1,0:T(8,128)(2,1)S(1)}, u32[]{:S(2)}, u32[]{:S(2)}) async-start(bf16[8,80,128]{2,1,0:T(8,128)(2,1)} %spread.1), calls=%async_computation.1 | async-start | bytes 327680 | tf_op jit(solution)/shard_map/all_to_all | solution.py:321
  60.2 13.0 %all-to-all-start.3 = ((bf16[8,296,128]{2,1,0:T(8,128)(2,1)}), bf16[8,296,128]{2,1,0:T(8,128)(2,1)S(1)}, u32[]{:S(2)}, u32[]{:S(2)}) async-start(bf16[8,296,128]{2,1,0:T(8,128)(2,1)} %combine.1), calls=%async_computation.3 | async-start | bytes 1212416 | tf_op jit(solution)/shard_map/all_to_all | solution.py:321

commit v8 on v7

--- a/solution.py
+++ b/solution.py
@@ -145,7 +145,7 @@
     )
     stats = pack_stats(joint_max, joint_sum)
     joint_out = joint_out.astype(BF16)
-    anchor = sums_ref[peers // 2, 2 * PROWS : 2 * PROWS + piece]
+    anchor = sums_ref[1, 2 * PROWS : 2 * PROWS + piece]
     for peer in range(peers):
         out_ref[peer, 0:QROWS] = joint_out
         out_ref[peer, QROWS : QROWS + SROWS] = stats
@@ -307,12 +307,14 @@
 
 def groups_of(contexts):
     far = contexts // NEAR
+    middle = far // 2
 
     def index(x, zz, zo):
-        x, zz = (x + HK // 2) % HK, (zz + far // 2) % far
         return (x * far + zz) * PARITIES + zo
 
-    xs, zzs, zos = range(HK), range(far), range(PARITIES)
+    xs, zos = [(x + HK // 2) % HK for x in range(HK)], range(PARITIES)
+    rest = [zz for zz in range(far) if zz != middle]
+    zzs = [middle] + sorted(rest, key=lambda zz: min(zz, far - zz))
     near = [[index(x, zz, zo) for x in xs for zo in zos] for zz in zzs]
     return near, [[index(x, zz, zo) for zz in zzs] for x in xs for zo in zos]
 
@@ -353,6 +355,7 @@
         own_kernel,
         (shape((HQ, HS, block), BF16), shape((HQ, 2, block), F32)),
         name="own",
+        compiler_params=pltpu.CompilerParams(),
         grid=(HK,),
         in_specs=[group_cols, head_cols, head_cols],
     )(ctx_query, ctx_key, ctx_value)

time: 78.6 us -> 78.1 us (level)
  starting transfers between devices: 24 us -> 23.2 us
    all_to_all x2, starting transfers between devices: 24 us -> 23.2 us  [exchange(): lax.all_to_all(value, 'ctx', 0, 0, axis_index_groups=groups, tiled=True)]
where the time goes in v8:
time: 78.1 us; the launch traced here: 77.7 us
  blocking collectives  31.8 us (41%)
  starting transfers between devices  23.2 us (30%)
  Pallas kernels  14.5 us (19%)
  waiting for transfers between devices  7.42 us (10%)
    all_to_all x2, blocking collectives, exchange(): lax.all_to_all(value, 'ctx', 0, 0, axis_index_groups=groups, tiled=True)  31.8 us
    all_to_all x2, starting transfers between devices, exchange(): lax.all_to_all(value, 'ctx', 0, 0, axis_index_groups=groups, tiled=True)  23.2 us
    all_to_all x2, waiting for transfers between devices, exchange(): lax.all_to_all(value, 'ctx', 0, 0, axis_index_groups=groups, tiled=True)  7.42 us
    pallas_call x1, Pallas kernels, layer(): call(own_kernel, (shape((HQ, HS, block), BF16), shape((HQ, 2, block), F32...  5.38 us
    pallas_call x1, Pallas kernels, layer(): pl.pallas_call(prefill_kernel, out_shape=(shape((block, HQ * HS), BF16),...  4.88 us
  transfers between devices with their start and end apart: 2, of which 2 were waited for; matrix products, arithmetic and copies ran while one was open for 0% of the time, Pallas kernels for 7%

profile of v8, /device:TPU:24, one launch (start us, length us, event | category | flops | bytes accessed | tf_op | source)
XLA Modules:
  0.0 77.7 jit_solution(4473955990035353563)
XLA Ops:
  0.6 1.5 %project.1 = bf16[8,304,128]{2,1,0:T(8,128)(2,1)S(1)} custom-call(bf16[4,64]{1,0:T(4,128)(2,1)} %embed_ref.1, bf16[64,2048]{1,0:T(8,128)(2,1)} %wq_ref.1, bf16[64,512]{1,0:T(8,128)(2,1)} %wk_ref.1, bf16[64,512]{1,0:T(8,128)(2,1)} %wv_ref.1, bf16[256,512]{1,0:T(8,128)(2,1)} %key_ref.3, bf16[256,512]{1,0:T(8,128)(2,1)} %value_ref.3), custom_call_target="tpu_custom_call" | custom-call | tf_op jit(solution)/shard_map/project/pallas_call | solution.py:336
  2.1 15.2 %all_to_all.20.in_ref.cache_ref = bf16[8,304,128]{2,1,0:T(8,128)(2,1)S(1)} all-to-all(bf16[8,304,128]{2,1,0:T(8,128)(2,1)S(1)} %project.1), channel_id=1, replica_groups={{40,41,56,57,8,9,24,25},{32,33,48,49,0,1,16,17},{34,35,50,51,2,3,18,19}..., dimensions={0} | all-to-all | bytes 1245184 | tf_op jit(solution)/shard_map/all_to_all | solution.py:323
  17.2 0.7 spread.1
  17.9 17.5 %all-to-all-start.1 = ((bf16[8,80,128]{2,1,0:T(8,128)(2,1)}), bf16[8,80,128]{2,1,0:T(8,128)(2,1)S(1)}, u32[]{:S(2)}, u32[]{:S(2)}) async-start(bf16[8,80,128]{2,1,0:T(8,128)(2,1)} %spread.1), calls=%async_computation.1 | async-start | bytes 327680 | tf_op jit(solution)/shard_map/all_to_all | solution.py:323
  35.5 0.1 negate_select_fusion
  35.6 6.4 %all-to-all-done.1.sums_ref = bf16[8,80,128]{2,1,0:T(8,128)(2,1)S(1)} async-done(((bf16[8,80,128]{2,1,0:T(8,128)(2,1)}), bf16[8,80,128]{2,1,0:T(8,128)(2,1)S(1)}, u32[]{:S(2)}, u32[]{:S(2)}) %all-to-all-start.1) | async-done | bytes 163872 | tf_op jit(solution)/shard_map/all_to_all | solution.py:323
  42.0 0.9 %decode.1 = (bf16[8,56,128]{2,1,0:T(8,128)(2,1)S(1)}, f32[3,16,128]{2,1,0:T(8,128)S(1)}) custom-call(bf16[8,80,128]{2,1,0:T(8,128)(2,1)S(1)} %all-to-all-done.1.sums_ref, bf16[8,304,128]{2,1,0:T(8,128)(2,1)S(1)} %all_to_all.20.in_ref.cache_ref, f32[24,128]{1,0:T(8,128)S(1)} %get-tuple-element.11.cos_ref, f32[24,128]{1,0:T(8,128)S(1)} %get-tuple-element.10.sin_ref), custom_call_target="tpu_custom_call" | custom-call | tf_op jit(solution)/shard_map/decode/pallas_call | solution.py:362
  42.8 16.6 %all_to_all.21.parts_ref = bf16[8,56,128]{2,1,0:T(8,128)(2,1)S(1)} all-to-all(bf16[8,56,128]{2,1,0:T(8,128)(2,1)S(1)} %get-tuple-element.8), channel_id=1, replica_groups={{40,32,34,46,36,44,38,42},{41,33,35,47,37,45,39,43},{56,48,50,62,52,60,..., dimensions={0} | all-to-all | bytes 229376 | tf_op jit(solution)/shard_map/all_to_all | solution.py:323
  59.4 1.2 %combine.1 = bf16[8,296,128]{2,1,0:T(8,128)(2,1)} custom-call(bf16[8,56,128]{2,1,0:T(8,128)(2,1)S(1)} %all_to_all.21.parts_ref, f32[3,16,128]{2,1,0:T(8,128)S(1)} %get-tuple-element.9.new_ref), custom_call_target="tpu_custom_call" | custom-call | tf_op jit(solution)/shard_map/combine/pallas_call | solution.py:369
  60.7 5.7 %all-to-all-start.3 = ((bf16[8,296,128]{2,1,0:T(8,128)(2,1)}), bf16[8,296,128]{2,1,0:T(8,128)(2,1)S(1)}, u32[]{:S(2)}, u32[]{:S(2)}) async-start(bf16[8,296,128]{2,1,0:T(8,128)(2,1)} %combine.1), calls=%async_computation.3 | async-start | bytes 1212416 | tf_op jit(solution)/shard_map/all_to_all | solution.py:323
  66.4 5.4 %own.1 = (bf16[16,128,256]{2,1,0:T(8,128)(2,1)S(1)}, f32[16,2,256]{2,1,0:T(2,128)S(1)}) custom-call(bf16[256,2048]{1,0:T(8,128)(2,1)} %query_ref.3, bf16[256,512]{1,0:T(8,128)(2,1)} %key_ref.3, bf16[256,512]{1,0:T(8,128)(2,1)} %value_ref.3), custom_call_target="tpu_custom_call" | custom-call | tf_op jit(solution)/shard_map/own/pallas_call | solution.py:354
  71.8 1.1 %all-to-all-done.3.anchor_ref = bf16[8,296,128]{2,1,0:T(8,128)(2,1)S(1)} async-done(((bf16[8,296,128]{2,1,0:T(8,128)(2,1)}), bf16[8,296,128]{2,1,0:T(8,128)(2,1)S(1)}, u32[]{:S(2)}, u32[]{:S(2)}) %all-to-all-start.3) | async-done | bytes 606240 | tf_op jit(solution)/shard_map/all_to_all | solution.py:323
  72.8 4.9 %prefill.1 = (bf16[256,2048]{1,0:T(8,128)(2,1)}, bf16[4,2048]{1,0:T(4,128)(2,1)}) custom-call(bf16[256,2048]{1,0:T(8,128)(2,1)} %query_ref.3, bf16[16,128,256]{2,1,0:T(8,128)(2,1)S(1)} %get-tuple-element.6.own_ref, f32[16,2,256]{2,1,0:T(2,128)S(1)} %get-tuple-element.7.own_stats_ref, bf16[8,296,128]{2,1,0:T(8,128)(2,1)S(1)} %all-to-all-done.3.anchor_ref), custom_call_target="tpu_custom_call" | custom-call | tf_op jit(solution)/shard_map/prefill/pallas_call | solution.py:376
  (4 shorter events, 0.0 us)
Async XLA Ops:
  17.9 24.0 %all-to-all-start.1 = ((bf16[8,80,128]{2,1,0:T(8,128)(2,1)}), bf16[8,80,128]{2,1,0:T(8,128)(2,1)S(1)}, u32[]{:S(2)}, u32[]{:S(2)}) async-start(bf16[8,80,128]{2,1,0:T(8,128)(2,1)} %spread.1), calls=%async_computation.1 | async-start | bytes 327680 | tf_op jit(solution)/shard_map/all_to_all | solution.py:323
  60.7 12.2 %all-to-all-start.3 = ((bf16[8,296,128]{2,1,0:T(8,128)(2,1)}), bf16[8,296,128]{2,1,0:T(8,128)(2,1)S(1)}, u32[]{:S(2)}, u32[]{:S(2)}) async-start(bf16[8,296,128]{2,1,0:T(8,128)(2,1)} %combine.1), calls=%async_computation.3 | async-start | bytes 1212416 | tf_op jit(solution)/shard_map/all_to_all | solution.py:323
